TPU v7x, 512 devices: a whole 4x4x16 slice. The times are simulated.
512 devices in a mesh: wide: 128 (over z, x, core), narrow: 4 (over y).
Axes of the slice: x: 4, y: 4, z: 16, core: 2. Of those that a mesh axis runs over, the one named last changes fastest.
Arguments:
- totals: float32 [16, 4096, 512], P('narrow', 'wide'), may hold values from 0.5 to 2
- courant: float32 [4096, 512], P('wide'), may hold values from 0.05 to 0.4
- diffusion: float32 [4096, 512], P('wide'), may hold values from 0.02 to 0.14
- stoich: float32 [32, 16], replicated, may hold values from 0 to 0.5
- log_k: float32 [32], replicated, may hold values from -2 to 0
- mineral_stoich: float32 [12, 16], replicated, may hold values from 0 to 0.5
- mineral_log_k: float32 [12], replicated, may hold values from 0 to 2
- mineral_rate: float32 [12], replicated, may hold values from 0.05 to 1
- front_counts: int32 [128, 4], replicated, may hold values from 0 to 16, as said below
- mineral_flags: int32 [2048, 4], P('wide', 'narrow'), may hold values 0 or 1
Outputs:
- speciated: float32 [16, 4096, 512], P(None, 'wide', 'narrow')
Inputs may be any that keep to these rules, and one draw needn't show every extreme that they name: `front_counts`: some tile has all 16 of its blocks front.
All inputs are finite; a program needn't handle non-finite values. Where the computation divides by a largest or mean magnitude, that divisor is 1e-20 or more. No bound on the sum of `mineral_flags` on one device may be relied on, other than what follows from the above.
Results may differ from a plain program's by a relative error of at most 0.0003.
Values sent between devices are 32-bit elements; how exact they have to be, the bound alone decides.
No kernel may reach another device: no remote copies, remote signals or barrier semaphores. Data moves between devices by JAX's collectives and lax.ppermute only.
A program may use at most 64 MiB of HBM per device.

v0:
```python
import jax
import jax.numpy as jnp
from jax import lax
from jax.sharding import PartitionSpec as P

STEPS = 4
ITERS = 4


def extended(shard, sides, width):
    for axis, dim in sides:
        count, length = (lax.axis_size(axis), shard.shape[dim])
        up = [(i, (i + 1) % count) for i in range(count - 1)]
        down = [(j, i) for i, j in up]
        last = lax.slice_in_dim(shard, length - width, length, axis=dim)
        first = lax.slice_in_dim(shard, 0, width, axis=dim)
        before = lax.ppermute(last, axis, up)
        after = lax.ppermute(first, axis, down)
        shard = jnp.concatenate([before, shard, after], axis=dim)
    return shard


def advance(fields, upwind, downwind, courant, diffusion):
    beside = jnp.pad(fields, ((0, 0), (0, 0), (1, 1)))
    return (
        fields
        - courant * (fields - upwind)
        + diffusion * (upwind + downwind + (beside[:, :, :-2] + beside[:, :, 2:]) - 4.0 * fields)
    )


def pair_table(matrix):
    return (matrix[:, :, None] * matrix[:, None, :]).reshape(matrix.shape[0], -1).T


def solve_batch(jacobian, residual):
    order = residual.shape[0]
    matrix_rows = [jacobian[i] for i in range(order)]
    values = [residual[i] for i in range(order)]
    for pivot_index in range(order):
        pivot_row = matrix_rows[pivot_index]
        for target in range(pivot_index + 1, order):
            factor = matrix_rows[target][pivot_index] / pivot_row[pivot_index]
            matrix_rows[target] = matrix_rows[target] - factor[None, :] * pivot_row
            values[target] = values[target] - factor * values[pivot_index]
    solution = [None] * order
    for pivot_index in reversed(range(order)):
        partial_sum = values[pivot_index]
        for column in range(pivot_index + 1, order):
            partial_sum = partial_sum - matrix_rows[pivot_index][column] * solution[column]
        solution[pivot_index] = partial_sum / matrix_rows[pivot_index][pivot_index]
    return jnp.stack(solution)


def speciate(
    total,
    mineral_on,
    stoich,
    log_k,
    mineral_stoich,
    mineral_log_k,
    mineral_rate,
    pair_sec,
    pair_min,
):
    highest = lax.Precision.HIGHEST
    order = total.shape[0]
    free_log = jnp.log(total)
    for repeat in range(ITERS):
        free_conc = jnp.exp(free_log)
        secondary = jnp.exp(log_k[:, None] + jnp.dot(stoich, free_log, precision=highest))
        saturation = mineral_rate[:, None] * jnp.exp(
            jnp.dot(mineral_stoich, free_log, precision=highest) - mineral_log_k[:, None]
        )
        residual = (
            free_conc
            + jnp.dot(stoich.T, secondary, precision=highest)
            + mineral_on * jnp.dot(mineral_stoich.T, saturation, precision=highest)
            - total
        )
        jacobian = jnp.dot(pair_sec, secondary, precision=highest) + mineral_on * jnp.dot(
            pair_min, saturation, precision=highest
        )
        jacobian = (
            jacobian.reshape(order, order, -1)
            + jnp.eye(order, dtype=jnp.float32)[:, :, None] * free_conc[:, None, :]
        )
        newton_step = solve_batch(jacobian, residual)
        largest = jnp.max(jnp.abs(newton_step), axis=0)
        free_log = free_log - newton_step / jnp.maximum(largest, 1.0)
    return free_log


def shards(
    totals,
    courant,
    diffusion,
    stoich,
    log_k,
    mineral_stoich,
    mineral_log_k,
    mineral_rate,
    front_counts,
    mineral_flags,
):
    rows_x = totals.shape[1]
    fields = totals
    for repeat in range(STEPS):
        padded = extended(fields, (("wide", 1),), 1)
        fields = advance(fields, padded[:, :-2], padded[:, 2:], courant, diffusion)
    regrouped = lax.all_to_all(fields, "narrow", split_axis=2, concat_axis=0, tiled=True)
    components, rows_x, width_y = regrouped.shape
    block_count = rows_x // 2
    blocks = regrouped.reshape(components, block_count, 2 * width_y)
    initial = jnp.log(blocks)
    flag_values = mineral_flags.reshape(block_count).astype(jnp.float32)
    own_count = front_counts[lax.axis_index("wide"), lax.axis_index("narrow")]
    pair_sec = pair_table(stoich)
    pair_min = pair_table(mineral_stoich)

    def visit(number, current):
        block_totals = lax.dynamic_slice_in_dim(blocks, number, 1, 1)[:, 0]
        mineral_on = lax.dynamic_index_in_dim(flag_values, number, 0, keepdims=False)
        solved = speciate(
            block_totals,
            mineral_on,
            stoich,
            log_k,
            mineral_stoich,
            mineral_log_k,
            mineral_rate,
            pair_sec,
            pair_min,
        )
        return lax.dynamic_update_slice_in_dim(current, solved[:, None], number, 1)

    result = lax.fori_loop(0, own_count, visit, initial)
    return result.reshape(components, rows_x, width_y)


def solution(mesh):
    placed = (
        P("narrow", "wide", None),
        P("wide", None),
        P("wide", None),
        P(),
        P(),
        P(),
        P(),
        P(),
        P(),
        P("wide", "narrow"),
    )
    return jax.shard_map(
        shards, mesh=mesh, in_specs=placed, out_specs=P(None, "wide", "narrow"), check_vma=False
    )
```

profile of v0, /device:TPU:152, one launch (start us, length us, event | category | flops | bytes accessed | tf_op | source)
XLA Modules:
  0.0 437.0 jit_solution(6493446748947393175)
XLA Ops:
  0.0 1.2 copy.69
  1.2 1.9 collective-permute-start
  3.1 7.0 %collective-permute-start.1 = (f32[4,1,512]{2,0,1:T(4,128)S(1)}, f32[4,1,512]{2,0,1:T(4,128)S(1)}, u32[]{:S(2)}, u32[]{:S(2)}) collective-permute-start(f32[4,1,512]{2,0,1:T(4,128)S(1)} %get-tuple-element.2462), channel_id=1, source_target_pairs={{4,0},{8,4},{12,8},{16,12},{20,16},{24,20},{28,24},{32,28},{36,32}... | collective-permute-start | bytes 24584 | tf_op jit(solution)/shard_map/ppermute | solution.py:18
  10.1 1.3 collective-permute-done.1
  11.8 1.9 collective-permute-start.2
  13.7 7.0 %collective-permute-start.3 = (f32[4,1,512]{2,0,1:T(4,128)S(1)}, f32[4,1,512]{2,0,1:T(4,128)S(1)}, u32[]{:S(2)}, u32[]{:S(2)}) collective-permute-start(f32[4,1,512]{2,0,1:T(4,128)S(1)} %get-tuple-element.2460), channel_id=1, source_target_pairs={{4,0},{8,4},{12,8},{16,12},{20,16},{24,20},{28,24},{32,28},{36,32}... | collective-permute-start | bytes 24584 | tf_op jit(solution)/shard_map/ppermute | solution.py:18
  20.7 1.3 collective-permute-done.3
  22.4 1.9 collective-permute-start.4
  24.4 7.0 %collective-permute-start.5 = (f32[4,1,512]{2,0,1:T(4,128)S(1)}, f32[4,1,512]{2,0,1:T(4,128)S(1)}, u32[]{:S(2)}, u32[]{:S(2)}) collective-permute-start(f32[4,1,512]{2,0,1:T(4,128)S(1)} %get-tuple-element.2458), channel_id=1, source_target_pairs={{4,0},{8,4},{12,8},{16,12},{20,16},{24,20},{28,24},{32,28},{36,32}... | collective-permute-start | bytes 24584 | tf_op jit(solution)/shard_map/ppermute | solution.py:18
  31.3 1.3 collective-permute-done.5
  33.1 1.9 collective-permute-start.6
  35.0 7.0 %collective-permute-start.7 = (f32[4,1,512]{2,0,1:T(4,128)S(1)}, f32[4,1,512]{2,0,1:T(4,128)S(1)}, u32[]{:S(2)}, u32[]{:S(2)}) collective-permute-start(f32[4,1,512]{2,0,1:T(4,128)S(1)} %get-tuple-element.2456), channel_id=1, source_target_pairs={{4,0},{8,4},{12,8},{16,12},{20,16},{24,20},{28,24},{32,28},{36,32}... | collective-permute-start | bytes 24584 | tf_op jit(solution)/shard_map/ppermute | solution.py:18
  42.0 1.3 dynamic_slice.10
  44.1 1.4 reshape.3426
  45.5 4.8 %all-to-all-start = ((f32[4,1,16384]{2,1,0:T(1,128)}), f32[4,1,16384]{2,1,0:T(1,128)S(1)}, u32[]{:S(2)}, u32[]{:S(2)}) async-start(f32[4,1,16384]{2,1,0:T(1,128)} %reshape.3426), calls=%async_computation | async-start | bytes 524288 | tf_op jit(solution)/shard_map/all_to_all | solution.py:111
  50.3 4.6 %all-to-all-done = f32[4,1,16384]{2,1,0:T(1,128)S(1)} async-done(((f32[4,1,16384]{2,1,0:T(1,128)}), f32[4,1,16384]{2,1,0:T(1,128)S(1)}, u32[]{:S(2)}, u32[]{:S(2)}) %all-to-all-start) | async-done | bytes 262176 | tf_op jit(solution)/shard_map/all_to_all | solution.py:111
  55.4 1.4 reduce
  58.5 377.7 %while.12 = (s32[]{:T(128)}, f32[16,16,256]{2,1,0:T(8,128)S(1)}, s32[]{:T(128)}, f32[16,16,256]{2,1,0:T(8,128)S(1)}, f32[32]{0:T(128)S(1)}, /*index=5*/f32[32,16...) while((s32[]{:T(128)}, f32[16,16,256]{2,1,0:T(8,128)S(1)}, ...), condition=%wide.region_5.6_spmd.clone.clone, body=%wide.region_0.5_spmd.clone.clone.sunk | while | flops 162068992 | bytes 30309204 | solution.py:137
  72.5 1.1 convolution_multiply_fusion.14
  96.1 1.1 convolution_multiply_fusion.14
  119.6 1.1 convolution_multiply_fusion.14
  143.2 1.1 convolution_multiply_fusion.14
  166.7 1.1 convolution_multiply_fusion.14
  190.3 1.1 convolution_multiply_fusion.14
  213.8 1.1 convolution_multiply_fusion.14
  237.4 1.1 convolution_multiply_fusion.14
  260.9 1.1 convolution_multiply_fusion.14
  284.5 1.1 convolution_multiply_fusion.14
  308.0 1.1 convolution_multiply_fusion.14
  331.5 1.1 convolution_multiply_fusion.14
  355.1 1.1 convolution_multiply_fusion.14
  378.6 1.1 convolution_multiply_fusion.14
  (4823 shorter events, 325.9 us)
Async XLA Ops:
  0.0 11.4 %copy-start.2 = (f32[32,512]{1,0:T(8,128)S(1)}, f32[32,512]{1,0:T(8,128)}, u32[]{:S(2)}) copy-start(f32[32,512]{1,0:T(8,128)} %param.14) | copy-start | bytes 196612
  0.0 11.4 %copy-start.3 = (f32[32,512]{1,0:T(8,128)S(1)}, f32[32,512]{1,0:T(8,128)}, u32[]{:S(2)}) copy-start(f32[32,512]{1,0:T(8,128)} %param.13) | copy-start | bytes 196612
  1.2 8.9 %collective-permute-start = (f32[4,1,512]{2,0,1:T(4,128)S(1)}, f32[4,1,512]{2,0,1:T(4,128)S(1)}, u32[]{:S(2)}, u32[]{:S(2)}) collective-permute-start(f32[4,1,512]{2,0,1:T(4,128)S(1)} %get-tuple-element.2461), channel_id=1, source_target_pairs={{0,4},{4,8},{8,12},{12,16},{16,20},{20,24},{24,28},{28,32},{32,36}... | collective-permute-start | bytes 24584 | tf_op jit(solution)/shard_map/ppermute | solution.py:17
  3.1 8.3 %collective-permute-start.1 = (f32[4,1,512]{2,0,1:T(4,128)S(1)}, f32[4,1,512]{2,0,1:T(4,128)S(1)}, u32[]{:S(2)}, u32[]{:S(2)}) collective-permute-start(f32[4,1,512]{2,0,1:T(4,128)S(1)} %get-tuple-element.2462), channel_id=1, source_target_pairs={{4,0},{8,4},{12,8},{16,12},{20,16},{24,20},{28,24},{32,28},{36,32}... | collective-permute-start | bytes 24584 | tf_op jit(solution)/shard_map/ppermute | solution.py:18
  11.8 8.9 %collective-permute-start.2 = (f32[4,1,512]{2,0,1:T(4,128)S(1)}, f32[4,1,512]{2,0,1:T(4,128)S(1)}, u32[]{:S(2)}, u32[]{:S(2)}) collective-permute-start(f32[4,1,512]{2,0,1:T(4,128)S(1)} %get-tuple-element.2459), channel_id=1, source_target_pairs={{0,4},{4,8},{8,12},{12,16},{16,20},{20,24},{24,28},{28,32},{32,36}... | collective-permute-start | bytes 24584 | tf_op jit(solution)/shard_map/ppermute | solution.py:17
  13.7 8.3 %collective-permute-start.3 = (f32[4,1,512]{2,0,1:T(4,128)S(1)}, f32[4,1,512]{2,0,1:T(4,128)S(1)}, u32[]{:S(2)}, u32[]{:S(2)}) collective-permute-start(f32[4,1,512]{2,0,1:T(4,128)S(1)} %get-tuple-element.2460), channel_id=1, source_target_pairs={{4,0},{8,4},{12,8},{16,12},{20,16},{24,20},{28,24},{32,28},{36,32}... | collective-permute-start | bytes 24584 | tf_op jit(solution)/shard_map/ppermute | solution.py:18
  22.4 8.9 %collective-permute-start.4 = (f32[4,1,512]{2,0,1:T(4,128)S(1)}, f32[4,1,512]{2,0,1:T(4,128)S(1)}, u32[]{:S(2)}, u32[]{:S(2)}) collective-permute-start(f32[4,1,512]{2,0,1:T(4,128)S(1)} %get-tuple-element.2457), channel_id=1, source_target_pairs={{0,4},{4,8},{8,12},{12,16},{16,20},{20,24},{24,28},{28,32},{32,36}... | collective-permute-start | bytes 24584 | tf_op jit(solution)/shard_map/ppermute | solution.py:17
  24.4 8.3 %collective-permute-start.5 = (f32[4,1,512]{2,0,1:T(4,128)S(1)}, f32[4,1,512]{2,0,1:T(4,128)S(1)}, u32[]{:S(2)}, u32[]{:S(2)}) collective-permute-start(f32[4,1,512]{2,0,1:T(4,128)S(1)} %get-tuple-element.2458), channel_id=1, source_target_pairs={{4,0},{8,4},{12,8},{16,12},{20,16},{24,20},{28,24},{32,28},{36,32}... | collective-permute-start | bytes 24584 | tf_op jit(solution)/shard_map/ppermute | solution.py:18
  33.1 10.2 %collective-permute-start.6 = (f32[4,1,512]{2,0,1:T(4,128)S(1)}, f32[4,1,512]{2,0,1:T(4,128)S(1)}, u32[]{:S(2)}, u32[]{:S(2)}) collective-permute-start(f32[4,1,512]{2,0,1:T(4,128)S(1)} %get-tuple-element.2455), channel_id=1, source_target_pairs={{0,4},{4,8},{8,12},{12,16},{16,20},{20,24},{24,28},{28,32},{32,36}... | collective-permute-start | bytes 24584 | tf_op jit(solution)/shard_map/ppermute | solution.py:17
  35.0 8.3 %collective-permute-start.7 = (f32[4,1,512]{2,0,1:T(4,128)S(1)}, f32[4,1,512]{2,0,1:T(4,128)S(1)}, u32[]{:S(2)}, u32[]{:S(2)}) collective-permute-start(f32[4,1,512]{2,0,1:T(4,128)S(1)} %get-tuple-element.2456), channel_id=1, source_target_pairs={{4,0},{8,4},{12,8},{16,12},{20,16},{24,20},{28,24},{32,28},{36,32}... | collective-permute-start | bytes 24584 | tf_op jit(solution)/shard_map/ppermute | solution.py:18
  45.5 4.8 %copy-start.4 = (s32[16,1]{0,1:T(1,128)S(1)}, s32[16,1]{0,1:T(1,128)}, u32[]{:S(2)}) copy-start(s32[16,1]{0,1:T(1,128)} %param.21) | copy-start | bytes 196
  45.5 9.4 %all-to-all-start = ((f32[4,1,16384]{2,1,0:T(1,128)}), f32[4,1,16384]{2,1,0:T(1,128)S(1)}, u32[]{:S(2)}, u32[]{:S(2)}) async-start(f32[4,1,16384]{2,1,0:T(1,128)} %reshape.3426), calls=%async_computation | async-start | bytes 524288 | tf_op jit(solution)/shard_map/all_to_all | solution.py:111
  57.7 0.7 copy-start
  57.7 0.7 copy-start.1
  57.8 0.7 copy-start.5
  57.8 0.7 copy-start.6
  57.8 0.7 copy-start.7
where the time goes:
time: 441 us; the launch traced here: 437 us
  matrix products  177 us (40%)
  other arithmetic  135 us (31%)
  loops' own time  41.8 us (9%)
  starting transfers between devices  40.3 us (9%)
  local copies, waits for them, and re-layouts  33.5 us (8%)
  waiting for transfers between devices  8.65 us (2%)
    dot_general x64, matrix products, speciate(): jnp.dot(pair_min, saturation, precision=highest)  67.8 us
    dot_general x64, matrix products, speciate(): jnp.dot(mineral_stoich.T, saturation, precision=highest)  54.3 us
    another operation x1, loops' own time, shards(): result = lax.fori_loop(0, own_count, visit, initial)  41.8 us
    sub x128, other arithmetic, solve_batch(): values[target] = values[target] - factor * values[pivot_index]  34.1 us
    div x192, other arithmetic, solve_batch(): solution[pivot_index] = partial_sum / matrix_rows[pivot_index][pivot_index]  33.1 us
    ppermute x4, starting transfers between devices, extended(): after = lax.ppermute(first, axis, down)  27.8 us
    sub x1344, other arithmetic, solve_batch(): matrix_rows[target] = matrix_rows[target] - factor[None, :] * pivot_row  24.4 us
    dot_general x64, matrix products, speciate(): jnp.dot(pair_sec, secondary, precision=highest)  22.1 us

commit v1 on v0

v1 whole, which is shorter than its diff:
```python
import functools
import jax, jax.numpy as jnp
from jax import lax
from jax.experimental import pallas as pl
from jax.experimental.pallas import tpu as pltpu
from jax.sharding import PartitionSpec as P

NC = 16
ROWS = 32
LANES = 128
ITERS = 4
STEPS = 4
KS = 48
PAIRS = [(i, j) for i in range(NC) for j in range(i, NC)]
PIDX = {p: n for n, p in enumerate(PAIRS)}
NP = len(PAIRS)
M2 = NP + NC


def split2(v):
    hi = v.astype(jnp.bfloat16)
    lo = (v - hi.astype(jnp.float32)).astype(jnp.bfloat16)
    return hi, lo


def speciate_kernel(idx_ref, counts_ref, flags_ref, at3_ref, a3_ref, bias_ref, rate_ref,
                    p0_ref, p1_ref, p2_ref, p3_ref, out_ref,
                    tot_ref, y_ref, jac_ref, l1_ref, l2_ref):
    me = idx_ref[1]
    count = counts_ref[idx_ref[0], me]
    a3 = a3_ref[...]
    hi, lo = split2(a3)
    lane = lax.broadcasted_iota(jnp.int32, a3.shape, 1)
    l1_ref[...] = jnp.where(lane < 2 * NC, hi.astype(jnp.float32), lo.astype(jnp.float32)).astype(jnp.bfloat16)
    at3 = at3_ref[...]
    row = 0
    for i in range(NC + 1):
        tab = at3[i:, :] * at3[i:i + 1, :] if i < NC else at3
        n = tab.shape[0]
        l2_ref[row:row + n, :] = tab
        row += n
    tab = l2_ref[...]
    hi, lo = split2(tab)
    lane = lax.broadcasted_iota(jnp.int32, tab.shape, 1)
    l2 = jnp.where(lane < 2 * KS, hi.astype(jnp.float32), lo.astype(jnp.float32)).astype(jnp.bfloat16)
    l1 = l1_ref[...]
    for k, part in enumerate((p0_ref, p1_ref, p2_ref, p3_ref)):
        base = pl.multiple_of(lax.rem(me - k + 4, 4) * (4 * ROWS), 4 * ROWS)
        val = part[...]
        tot_ref[pl.ds(base, 4 * ROWS), :] = val
        y_ref[pl.ds(base, 4 * ROWS), :] = jnp.log(val)

    def stage(g):
        ys = jnp.concatenate([y_ref[pl.ds(8 * g + r, NC, stride=ROWS), :] for r in range(8)], axis=1)
        y1, y2 = split2(ys)
        s = jnp.dot(l1, jnp.concatenate([y1, y2, y1], axis=0), preferred_element_type=jnp.float32)
        xs = []
        for r in range(8):
            x = jnp.exp(s[:, r * LANES:(r + 1) * LANES] + bias_ref[...])
            m = flags_ref[(8 * g + r) // 2, 0].astype(jnp.float32)
            xs.append(jnp.concatenate([x[:32], x[32:] * (rate_ref[...] * m)], axis=0))
        x1, x2 = split2(jnp.concatenate(xs, axis=1))
        gm = jnp.dot(l2, jnp.concatenate([x1, x2, x1], axis=0), preferred_element_type=jnp.float32)
        for r in range(8):
            jac_ref[pl.ds(8 * g + r, M2, stride=ROWS), :] = gm[:, r * LANES:(r + 1) * LANES]

    def solve(g):
        def jac(p):
            return jac_ref[p * ROWS + 8 * g:p * ROWS + 8 * g + 8, :]
        def cell(ref, k):
            return ref[k * ROWS + 8 * g:k * ROWS + 8 * g + 8, :]
        w = [[None] * NC for _ in range(NC + 1)]
        rd = [None] * NC
        for j in range(NC):
            lj = [w[j][k] * rd[k] for k in range(j)]
            cj = jnp.exp(cell(y_ref, j))
            for i in range(j, NC + 1):
                if i == NC:
                    acc = jac(NP + j) + cj - cell(tot_ref, j)
                else:
                    acc = jac(PIDX[(j, i)])
                    if i == j:
                        acc = acc + cj
                for k in range(j):
                    acc = acc - w[i][k] * lj[k]
                w[i][j] = acc
            rd[j] = 1.0 / w[j][j]
        sol = [None] * NC
        for j in reversed(range(NC)):
            acc = w[NC][j]
            for i in range(j + 1, NC):
                acc = acc - w[i][j] * sol[i]
            sol[j] = acc * rd[j]
        largest = functools.reduce(jnp.maximum, [jnp.abs(v) for v in sol])
        scale = 1.0 / jnp.maximum(largest, 1.0)
        for j in range(NC):
            y_ref[j * ROWS + 8 * g:j * ROWS + 8 * g + 8, :] = cell(y_ref, j) - sol[j] * scale

    stage(0)

    def body(it, carry):
        for g in range(4):
            stage((g + 1) % 4)
            solve(g)
        return carry

    lax.fori_loop(0, ITERS, body, 0)
    for g in range(4):
        front = 8 * g + lax.broadcasted_iota(jnp.int32, (8, LANES), 0) < 2 * count
        for k in range(NC):
            sl = slice(k * ROWS + 8 * g, k * ROWS + 8 * g + 8)
            out_ref[sl, :] = jnp.where(front, y_ref[sl, :], jnp.log(tot_ref[sl, :]))


def tables(stoich, log_k, mineral_stoich, mineral_log_k, mineral_rate):
    nsec, nm = stoich.shape[0], mineral_stoich.shape[0]
    a = jnp.concatenate([stoich, mineral_stoich, jnp.zeros((KS - nsec - nm, NC), jnp.float32)], axis=0)
    a3 = jnp.concatenate([a, a, a], axis=1)
    at = a.T
    at3 = jnp.concatenate([at, at, at], axis=1)
    bias = jnp.concatenate([log_k, -mineral_log_k, jnp.zeros((KS - nsec - nm,), jnp.float32)])
    rate = jnp.concatenate([mineral_rate, jnp.zeros((KS - nsec - nm,), jnp.float32)])
    return at3, a3, jnp.broadcast_to(bias[:, None], (KS, LANES)), jnp.broadcast_to(rate[:, None], (16, LANES))


def speciate(idx, counts, flags, tabs, parts):
    smem = pl.BlockSpec(memory_space=pltpu.SMEM)
    vmem = pl.BlockSpec(memory_space=pltpu.VMEM)
    return pl.pallas_call(
        speciate_kernel,
        out_shape=jax.ShapeDtypeStruct((NC * ROWS, LANES), jnp.float32),
        in_specs=[smem] * 3 + [vmem] * 8,
        out_specs=vmem,
        scratch_shapes=[
            pltpu.VMEM((NC * ROWS, LANES), jnp.float32),
            pltpu.VMEM((NC * ROWS, LANES), jnp.float32),
            pltpu.VMEM((M2 * ROWS, LANES), jnp.float32),
            pltpu.VMEM((KS, 3 * NC), jnp.bfloat16),
            pltpu.VMEM((M2, 3 * KS), jnp.float32),
        ],
        name="speciate",
    )(idx, counts, flags, *tabs, *parts)


HALO = 4


def transport_kernel(idx_ref, before_ref, after_ref, tot_ref, cour_ref, diff_ref,
                     o0_ref, o1_ref, o2_ref, o3_ref, ext_ref, fin_ref):
    width = ext_ref.shape[1]
    zeros = jnp.zeros((4, width), jnp.float32)
    ext_ref[0:4, :] = zeros
    ext_ref[44:48, :] = zeros

    def extend(own, part):
        ext_ref[4:8, :] = before_ref[part]
        ext_ref[8:40, :] = own
        ext_ref[40:44, :] = after_ref[part]
        return ext_ref[...]

    courant = extend(cour_ref[...], 4)
    diffusion = extend(diff_ref[...], 5)
    keep = 1.0 - courant - 4.0 * diffusion
    behind = courant + diffusion
    col = lax.broadcasted_iota(jnp.int32, (48, width), 1)
    for c in range(4):
        f = extend(tot_ref[c], c)
        for step in range(STEPS):
            up = pltpu.roll(f, 1, 0)
            down = pltpu.roll(f, 47, 0)
            left = jnp.where(col == 0, 0.0, pltpu.roll(f, 1, 1))
            right = jnp.where(col == width - 1, 0.0, pltpu.roll(f, width - 1, 1))
            f = keep * f + behind * up + diffusion * (down + (left + right))
        fin_ref[c * ROWS:(c + 1) * ROWS, :] = f[8:40, :]
    me = idx_ref[1]
    for k, out_ref in enumerate((o0_ref, o1_ref, o2_ref, o3_ref)):
        start = pl.multiple_of(lax.rem(me + k, 4) * LANES, LANES)
        out_ref[...] = fin_ref[:, pl.ds(start, LANES)]


def transport(idx, before, after, totals, courant, diffusion):
    smem = pl.BlockSpec(memory_space=pltpu.SMEM)
    vmem = pl.BlockSpec(memory_space=pltpu.VMEM)
    width = totals.shape[2]
    return pl.pallas_call(
        transport_kernel,
        out_shape=[jax.ShapeDtypeStruct((4 * ROWS, LANES), jnp.float32)] * 4,
        in_specs=[smem] + [vmem] * 5,
        out_specs=[vmem] * 4,
        scratch_shapes=[
            pltpu.VMEM((48, width), jnp.float32),
            pltpu.VMEM((4 * ROWS, width), jnp.float32),
        ],
        name="transport",
    )(idx, before, after, totals, courant, diffusion)


def shards(totals, courant, diffusion, stoich, log_k, mineral_stoich, mineral_log_k,
           mineral_rate, front_counts, mineral_flags):
    idx = jnp.stack([lax.axis_index("wide"), lax.axis_index("narrow")]).astype(jnp.int32)
    count = lax.axis_size("wide")
    up = [(i, i + 1) for i in range(count - 1)]
    down = [(i + 1, i) for i in range(count - 1)]

    def rows(start, stop):
        return jnp.concatenate(
            [totals[:, start:stop], courant[None, start:stop], diffusion[None, start:stop]], axis=0)

    before = lax.ppermute(rows(ROWS - HALO, ROWS), "wide", up)
    after = lax.ppermute(rows(0, HALO), "wide", down)
    own = transport(idx, before, after, totals, courant, diffusion)
    parts = [own[0]]
    for k in (1, 2, 3):
        parts.append(lax.ppermute(own[k], "narrow", [(i, (i + k) % 4) for i in range(4)]))
    tabs = tables(stoich, log_k, mineral_stoich, mineral_log_k, mineral_rate)
    out = speciate(idx, front_counts, mineral_flags, tabs, parts)
    return out.reshape(NC, ROWS, LANES)


def solution(mesh):
    placed = (
        P("narrow", "wide", None), P("wide", None), P("wide", None),
        P(), P(), P(), P(), P(), P(), P("wide", "narrow"),
    )
    return jax.shard_map(
        shards, mesh=mesh, in_specs=placed, out_specs=P(None, "wide", "narrow"), check_vma=False
    )
```

time: 441 us -> 54.5 us (0.12)
  the two profiles are of different devices: /device:TPU:152 before, /device:TPU:384 now
where the time goes in v1:
time: 54.5 us; the launch traced here: 54 us
  Pallas kernels  20.6 us (38%)
  starting transfers between devices  20.4 us (37%)
  local copies, waits for them, and re-layouts  7.82 us (14%)
  waiting for transfers between devices  2.99 us (5%)
  other arithmetic  2.05 us (4%)
    pallas_call x1, Pallas kernels, speciate(): pl.pallas_call(speciate_kernel, out_shape=jax.ShapeDtypeStruct((NC * ROWS...  17.3 us
    ppermute x3, starting transfers between devices, shards(): lax.ppermute(own[k], 'narrow', [(i, (i + k) % 4) for i in range(4)])  11.5 us
    ppermute x1, starting transfers between devices, shards(): after = lax.ppermute(rows(0, HALO), 'wide', down)  6.96 us
    unnamed x27, local copies, waits for them, and re-layouts  4.75 us
    pallas_call x1, Pallas kernels, transport(): pl.pallas_call(transport_kernel, out_shape=[jax.ShapeDtypeStruct((4 * ROW...  3.24 us
    ppermute x3, waiting for transfers between devices, shards(): lax.ppermute(own[k], 'narrow', [(i, (i + k) % 4) for i in range(4)])  2.99 us
    ppermute x1, starting transfers between devices, shards(): before = lax.ppermute(rows(ROWS - HALO, ROWS), 'wide', up)  1.92 us
  transfers between devices with their start and end apart: 5, of which 1 were waited for; matrix products, arithmetic and copies ran while one was open for 7% of the time, Pallas kernels for 0%

profile of v1, /device:TPU:384, one launch (start us, length us, event | category | flops | bytes accessed | tf_op | source)
XLA Modules:
  0.0 54.0 jit_solution(2316436555381050177)
XLA Ops:
  0.0 0.9 %fusion = (f32[4,4,512]{2,1,0:T(4,128)S(1)}, f32[4,4,512]{2,1,0:T(4,128)S(1)}) fusion(f32[4,32,512]{2,1,0:T(8,128)} %tot_ref.1), kind=kLoop, calls=%fused_computation.11 | loop fusion | bytes 131072 | tf_op jit(solution)/shard_map/slice | solution.py:207
  0.9 0.8 %slice_bitcast_fusion = (f32[1,4,512]{2,1,0:T(4,128)S(1)}, f32[1,4,512]{2,1,0:T(4,128)S(1)}, f32[1,4,512]{2,1,0:T(4,128)S(1)}, f32[1,4,512]{2,1,0:T(4,128)S(1)}) fusion(f32[32,512]{1,0:T(8,128)} %diff_ref.1, f32[32,512]{1,0:T(8,128)} %cour_ref.1), kind=kLoop, calls=%fused_computation.5 | loop fusion | bytes 65536 | tf_op jit(solution)/shard_map/broadcast_in_dim | solution.py:207
  1.7 1.9 %collective-permute-start = (f32[6,4,512]{2,1,0:T(4,128)S(1)}, f32[6,4,512]{2,1,0:T(4,128)S(1)}, u32[]{:S(2)}, u32[]{:S(2)}) collective-permute-start(f32[6,4,512]{2,1,0:T(4,128)S(1)} %pad_maximum_fusion), channel_id=1, source_target_pairs={{0,4},{4,8},{8,12},{12,16},{16,20},{20,24},{24,28},{28,32},{32,36}... | collective-permute-start | bytes 147464 | tf_op jit(solution)/shard_map/ppermute | solution.py:209
  3.6 0.0 copy-start.6
  3.6 7.0 %collective-permute-start.1 = (f32[6,4,512]{2,1,0:T(4,128)S(1)}, f32[6,4,512]{2,1,0:T(4,128)S(1)}, u32[]{:S(2)}, u32[]{:S(2)}) collective-permute-start(f32[6,4,512]{2,1,0:T(4,128)S(1)} %pad_maximum_fusion.1), channel_id=1, source_target_pairs={{4,0},{8,4},{12,8},{16,12},{20,16},{24,20},{28,24},{32,28},{36,32}... | collective-permute-start | bytes 147464 | tf_op jit(solution)/shard_map/ppermute | solution.py:210
  10.6 0.0 copy-start.5
  10.6 0.1 copy.21
  10.7 0.6 %copy-done.5 = f32[12,16]{1,0:T(8,128)S(1)} copy-done((f32[12,16]{1,0:T(8,128)S(1)}, f32[12,16]{1,0:T(8,128)}, u32[]{:S(2)}) %copy-start.5) | copy-done | bytes 792
  11.3 0.7 %maximum_maximum_fusion.a3_ref = f32[48,48]{1,0:T(8,128)} fusion(f32[4,16]{1,0:T(4,128)S(1)} %broadcast_in_dim.27, f32[12,16]{1,0:T(8,128)S(1)} %copy-done.5, f32[32,16]{1,0:T(8,128)S(1)} %copy.21), kind=kLoop, calls=%fused_computation.3 | loop fusion | flops 18432 | bytes 12288 | tf_op jit(solution)/shard_map/concatenate | solution.py:118
  12.0 0.1 copy.22
  12.1 0.7 %pad_maximum_fusion.2.at3_ref = f32[16,144]{1,0:T(8,128)} fusion(f32[16,48]{1,0:T(8,128)S(1)} %copy.22), kind=kLoop, calls=%fused_computation.4 | loop fusion | flops 4608 | bytes 12288 | tf_op jit(solution)/shard_map/concatenate | solution.py:120
  12.8 0.6 %pad_add_fusion.idx_ref = s32[2]{0:T(128)} fusion(s32[1]{0:T(128)} %bitcast.1, s32[1]{0:T(128)} %bitcast), kind=kLoop, calls=%fused_computation.9 | loop fusion | flops 2 | bytes 16 | tf_op jit(solution)/shard_map/stack | solution.py:200
  13.3 0.1 copy-done.10
  13.4 0.7 %copy-done.11 = f32[12]{0:T(128)S(1)} copy-done((f32[12]{0:T(128)S(1)}, f32[12]{0:T(128)}, u32[]{:S(2)}) %copy-start.11) | copy-done | bytes 72
  14.1 0.6 %copy-done.8 = s32[16,1]{0,1:T(1,128)S(1)} copy-done((s32[16,1]{0,1:T(1,128)S(1)}, s32[16,1]{0,1:T(1,128)}, u32[]{:S(2)}) %copy-start.8) | copy-done | bytes 88
  14.8 0.7 %copy.26.flags_ref = s32[16,1]{1,0:T(8,128)} copy(s32[16,1]{0,1:T(1,128)S(1)} %copy-done.8) | data formatting | bytes 128 | tf_op args[9]
  15.4 0.0 copy-done.7
  15.4 0.7 %copy.25.counts_ref = s32[128,4]{1,0:T(8,128)} copy(s32[128,4]{0,1:T(4,128)S(1)} %copy-done.7) | data formatting | bytes 4096 | tf_op args[8]
  16.2 0.0 collective-permute-done.before_ref
  16.2 0.6 %copy-done.3 = f32[6,4,512]{2,1,0:T(4,128)} copy-done((f32[6,4,512]{2,1,0:T(4,128)}, f32[6,4,512]{2,1,0:T(4,128)S(1)}, u32[]{:S(2)}) %copy-start.3) | copy-done | bytes 49176
  16.8 0.6 %copy-done.4 = f32[6,4,512]{2,1,0:T(4,128)} copy-done((f32[6,4,512]{2,1,0:T(4,128)}, f32[6,4,512]{2,1,0:T(4,128)S(1)}, u32[]{:S(2)}) %copy-start.4) | copy-done | bytes 49176
  17.4 3.2 %transport.1 = (f32[128,128]{1,0:T(8,128)}, f32[128,128]{1,0:T(8,128)}, f32[128,128]{1,0:T(8,128)}, f32[128,128]{1,0:T(8,128)}) custom-call(s32[2]{0:T(128)} %pad_add_fusion.idx_ref, f32[6,4,512]{2,1,0:T(4,128)} %copy-done.3, f32[6,4,512]{2,1,0:T(4,128)} %copy-done.4, f32[4,32,512]{2,1,0:T(8,128)} %tot_ref.1, f32[32,512]{1,0:T(8,128)} %cour_ref.1, ...), custom_call_target="tpu_custom_call" | custom-call | tf_op jit(solution)/shard_map/transport/pallas_call | solution.py:185
  20.6 3.5 %collective-permute-start.2 = (f32[128,128]{1,0:T(8,128)}, f32[128,128]{1,0:T(8,128)S(1)}, u32[]{:S(2)}, u32[]{:S(2)}) collective-permute-start(f32[128,128]{1,0:T(8,128)} %get-tuple-element.10), channel_id=1, source_target_pairs={{0,1},{1,2},{2,3},{3,0},{4,5},{5,6},{6,7},{7,4},{8,9},{9,10},{10,1... | collective-permute-start | bytes 196616 | tf_op jit(solution)/shard_map/ppermute | solution.py:214
  24.1 4.8 %collective-permute-start.3 = (f32[128,128]{1,0:T(8,128)}, f32[128,128]{1,0:T(8,128)S(1)}, u32[]{:S(2)}, u32[]{:S(2)}) collective-permute-start(f32[128,128]{1,0:T(8,128)} %get-tuple-element.11), channel_id=1, source_target_pairs={{0,2},{1,3},{2,0},{3,1},{4,6},{5,7},{6,4},{7,5},{8,10},{9,11},{10,... | collective-permute-start | bytes 196616 | tf_op jit(solution)/shard_map/ppermute | solution.py:214
  28.9 0.0 copy-start.9
  28.9 3.3 %collective-permute-start.4 = (f32[128,128]{1,0:T(8,128)}, f32[128,128]{1,0:T(8,128)S(1)}, u32[]{:S(2)}, u32[]{:S(2)}) collective-permute-start(f32[128,128]{1,0:T(8,128)} %get-tuple-element.12), channel_id=1, source_target_pairs={{0,3},{1,0},{2,1},{3,2},{4,7},{5,4},{6,5},{7,6},{8,11},{9,8},{10,9... | collective-permute-start | bytes 196616 | tf_op jit(solution)/shard_map/ppermute | solution.py:214
  32.2 0.1 pad_maximum_fusion.3
  32.3 0.0 collective-permute-done.2.p1_ref
  32.3 3.0 %collective-permute-done.4.p3_ref = f32[128,128]{1,0:T(8,128)S(1)} collective-permute-done((f32[128,128]{1,0:T(8,128)}, f32[128,128]{1,0:T(8,128)S(1)}, u32[]{:S(2)}, u32[]{:S(2)}) %collective-permute-start.4) | collective-permute-done | bytes 65568 | tf_op jit(solution)/shard_map/ppermute | solution.py:214
  35.3 0.7 %broadcast_in_dim.29.rate_ref = f32[16,128]{1,0:T(8,128)} broadcast(f32[16]{0:T(128)S(1)} %concatenate.25), dimensions={0} | broadcast | bytes 8256 | tf_op jit(solution)/shard_map/broadcast_in_dim | solution.py:123
  36.0 0.7 %broadcast_in_dim.28.bias_ref = f32[48,128]{1,0:T(8,128)} broadcast(f32[48]{0:T(128)S(1)} %pad_maximum_fusion.3), dimensions={0} | broadcast | bytes 24768 | tf_op jit(solution)/shard_map/broadcast_in_dim | solution.py:123
  36.7 17.3 %speciate.1 = f32[512,128]{1,0:T(8,128)} custom-call(s32[2]{0:T(128)} %pad_add_fusion.idx_ref, s32[128,4]{1,0:T(8,128)} %copy.25.counts_ref, s32[16,1]{1,0:T(8,128)} %copy.26.flags_ref, f32[16,144]{1,0:T(8,128)} %pad_maximum_fusion.2.at3_ref, f32[48,48]{1,0:T(8,128)} %maximum_maximum_fusion.a3_ref, f32[48,128]{1,0:T(8,128)} %broadcast_in_dim.28.bias_ref, ...), custom_call_target="tpu_custom_call" | custom-call | tf_op jit(solution)/shard_map/speciate/pallas_call | solution.py:129
  (23 shorter events, 0.1 us)
Async XLA Ops:
  1.7 14.5 %collective-permute-start = (f32[6,4,512]{2,1,0:T(4,128)S(1)}, f32[6,4,512]{2,1,0:T(4,128)S(1)}, u32[]{:S(2)}, u32[]{:S(2)}) collective-permute-start(f32[6,4,512]{2,1,0:T(4,128)S(1)} %pad_maximum_fusion), channel_id=1, source_target_pairs={{0,4},{4,8},{8,12},{12,16},{16,20},{20,24},{24,28},{28,32},{32,36}... | collective-permute-start | bytes 147464 | tf_op jit(solution)/shard_map/ppermute | solution.py:209
  3.6 7.0 %copy-start.6 = (f32[32,16]{0,1:T(8,128)S(1)}, f32[32,16]{0,1:T(8,128)}, u32[]{:S(2)}) copy-start(f32[32,16]{0,1:T(8,128)} %param.13) | copy-start | bytes 6148
  3.6 12.5 %collective-permute-start.1 = (f32[6,4,512]{2,1,0:T(4,128)S(1)}, f32[6,4,512]{2,1,0:T(4,128)S(1)}, u32[]{:S(2)}, u32[]{:S(2)}) collective-permute-start(f32[6,4,512]{2,1,0:T(4,128)S(1)} %pad_maximum_fusion.1), channel_id=1, source_target_pairs={{4,0},{8,4},{12,8},{16,12},{20,16},{24,20},{28,24},{32,28},{36,32}... | collective-permute-start | bytes 147464 | tf_op jit(solution)/shard_map/ppermute | solution.py:210
  10.6 0.7 %copy-start.5 = (f32[12,16]{1,0:T(8,128)S(1)}, f32[12,16]{1,0:T(8,128)}, u32[]{:S(2)}) copy-start(f32[12,16]{1,0:T(8,128)} %param.15) | copy-start | bytes 2308
  12.8 0.7 %copy-start.10 = (f32[12]{0:T(128)S(1)}, f32[12]{0:T(128)}, u32[]{:S(2)}) copy-start(f32[12]{0:T(128)} %param.16) | copy-start | bytes 148
  13.4 0.7 %copy-start.11 = (f32[12]{0:T(128)S(1)}, f32[12]{0:T(128)}, u32[]{:S(2)}) copy-start(f32[12]{0:T(128)} %param.17) | copy-start | bytes 148
  14.1 0.7 %copy-start.8 = (s32[16,1]{0,1:T(1,128)S(1)}, s32[16,1]{0,1:T(1,128)}, u32[]{:S(2)}) copy-start(s32[16,1]{0,1:T(1,128)} %param.19) | copy-start | bytes 196
  14.8 0.7 %copy-start.7 = (s32[128,4]{0,1:T(4,128)S(1)}, s32[128,4]{0,1:T(4,128)}, u32[]{:S(2)}) copy-start(s32[128,4]{0,1:T(4,128)} %param.18) | copy-start | bytes 6148
  16.2 0.6 %copy-start.3 = (f32[6,4,512]{2,1,0:T(4,128)}, f32[6,4,512]{2,1,0:T(4,128)S(1)}, u32[]{:S(2)}) copy-start(f32[6,4,512]{2,1,0:T(4,128)S(1)} %collective-permute-done.before_ref) | copy-start | bytes 147460
  16.8 0.6 %copy-start.4 = (f32[6,4,512]{2,1,0:T(4,128)}, f32[6,4,512]{2,1,0:T(4,128)S(1)}, u32[]{:S(2)}) copy-start(f32[6,4,512]{2,1,0:T(4,128)S(1)} %collective-permute-done.1.after_ref) | copy-start | bytes 147460
  20.6 11.7 %collective-permute-start.2 = (f32[128,128]{1,0:T(8,128)}, f32[128,128]{1,0:T(8,128)S(1)}, u32[]{:S(2)}, u32[]{:S(2)}) collective-permute-start(f32[128,128]{1,0:T(8,128)} %get-tuple-element.10), channel_id=1, source_target_pairs={{0,1},{1,2},{2,3},{3,0},{4,5},{5,6},{6,7},{7,4},{8,9},{9,10},{10,1... | collective-permute-start | bytes 196616 | tf_op jit(solution)/shard_map/ppermute | solution.py:214
  24.1 8.2 %collective-permute-start.3 = (f32[128,128]{1,0:T(8,128)}, f32[128,128]{1,0:T(8,128)S(1)}, u32[]{:S(2)}, u32[]{:S(2)}) collective-permute-start(f32[128,128]{1,0:T(8,128)} %get-tuple-element.11), channel_id=1, source_target_pairs={{0,2},{1,3},{2,0},{3,1},{4,6},{5,7},{6,4},{7,5},{8,10},{9,11},{10,... | collective-permute-start | bytes 196616 | tf_op jit(solution)/shard_map/ppermute | solution.py:214
  28.9 3.3 %copy-start.9 = (f32[32]{0:T(128)S(1)}, f32[32]{0:T(128)}, u32[]{:S(2)}) copy-start(f32[32]{0:T(128)} %param.14) | copy-start | bytes 388
  28.9 6.4 %collective-permute-start.4 = (f32[128,128]{1,0:T(8,128)}, f32[128,128]{1,0:T(8,128)S(1)}, u32[]{:S(2)}, u32[]{:S(2)}) collective-permute-start(f32[128,128]{1,0:T(8,128)} %get-tuple-element.12), channel_id=1, source_target_pairs={{0,3},{1,0},{2,1},{3,2},{4,7},{5,4},{6,5},{7,6},{8,11},{9,8},{10,9... | collective-permute-start | bytes 196616 | tf_op jit(solution)/shard_map/ppermute | solution.py:214
  32.3 4.3 %copy-start = (f32[128,128]{1,0:T(8,128)}, f32[128,128]{1,0:T(8,128)S(1)}, u32[]{:S(2)}) copy-start(f32[128,128]{1,0:T(8,128)S(1)} %collective-permute-done.2.p1_ref) | copy-start | bytes 196612
  32.3 4.3 %copy-start.1 = (f32[128,128]{1,0:T(8,128)}, f32[128,128]{1,0:T(8,128)S(1)}, u32[]{:S(2)}) copy-start(f32[128,128]{1,0:T(8,128)S(1)} %collective-permute-done.3.p2_ref) | copy-start | bytes 196612
  35.3 1.3 %copy-start.2 = (f32[128,128]{1,0:T(8,128)}, f32[128,128]{1,0:T(8,128)S(1)}, u32[]{:S(2)}) copy-start(f32[128,128]{1,0:T(8,128)S(1)} %collective-permute-done.4.p3_ref) | copy-start | bytes 196612

commit v2 on v1

v2 whole, which is shorter than its diff:
```python
import functools

import jax
import jax.numpy as jnp
from jax import lax
from jax.experimental import pallas as pl
from jax.experimental.pallas import tpu as pltpu
from jax.sharding import PartitionSpec as P

STEPS = 4
ITERS = 4
HALO = 4
CHUNK = 8
NC = 16
ROWS = 32
LANES = 128
NBLK = 16
NSEC = 32
NM = 12
KS = 48
OFF = -16384.0
PITCH = 33
LOG2E = 1.4426950408889634
LN2 = 0.6931471805599453
PAIRS = [(i, j) for i in range(NC) for j in range(i, NC)]
PIDX = {p: n for n, p in enumerate(PAIRS)}
NP = len(PAIRS)
M2 = NP + NC
HBM = pl.BlockSpec(memory_space=pl.ANY)
VMEM = pl.BlockSpec(memory_space=pltpu.VMEM)


def on_chip(x):
    return pltpu.with_memory_space_constraint(x, pltpu.VMEM)


def in_hbm(x):
    return pltpu.with_memory_space_constraint(x, pltpu.HBM)


def vmem_out(shape, dtype=jnp.float32):
    return pltpu.VMEM(shape, dtype)


def split2(v):
    hi = v.astype(jnp.bfloat16)
    lo = (v - hi.astype(jnp.float32)).astype(jnp.bfloat16)
    return hi, lo


def is_even():
    return lax.rem(lax.axis_index("wide"), 2) == 0


def pack_kernel(tot_ref, cour_ref, diff_ref, pair_ref, next_ref, edge_ref, sems):
    copies = []
    for side, start in enumerate((0, ROWS - 8)):
        for n, (src, dst) in enumerate((
            (tot_ref.at[:, start:start + 8, :], edge_ref.at[side, 0:4]),
            (cour_ref.at[start:start + 8, :], edge_ref.at[side, 4]),
            (diff_ref.at[start:start + 8, :], edge_ref.at[side, 5]),
        )):
            copies.append(pltpu.make_async_copy(src, dst, sems.at[3 * side + n]))
    for c in copies:
        c.start()
    for c in copies:
        c.wait()
    first = edge_ref[0, :, 0:HALO, :]
    last = edge_ref[1, :, 8 - HALO:8, :]
    even = is_even()
    pair_ref[...] = jnp.where(even, last, first)
    next_ref[...] = jnp.where(even, first, last)


def pack(totals, courant, diffusion):
    width = totals.shape[2]
    return pl.pallas_call(
        pack_kernel,
        out_shape=[vmem_out((6, HALO, width))] * 2,
        in_specs=[HBM] * 3,
        out_specs=[VMEM] * 2,
        scratch_shapes=[pltpu.VMEM((2, 6, 8, width), jnp.float32), pltpu.SemaphoreType.DMA((6,))],
        compiler_params=pltpu.CompilerParams(vmem_limit_bytes=4 << 20),
        name="pack",
    )(*[in_hbm(v) for v in (totals, courant, diffusion)])


def transport_kernel(pair_ref, next_ref, tot_ref, cour_ref, diff_ref, out_ref, buf_ref, coef_ref, res_ref, sems):
    tiles = buf_ref.shape[2]
    even = is_even()
    parts = [slice(k * LANES, (k + 1) * LANES) for k in range(tiles)]
    zeros = jnp.zeros((8, LANES), jnp.float32)
    for slot in range(2):
        for c in range(4):
            for k in range(tiles):
                buf_ref[slot, c, k, 0:8, :] = zeros
                buf_ref[slot, c, k, 48:56, :] = zeros

    def extend(dst, own, part):
        before = jnp.where(even, next_ref[part], pair_ref[part])
        after = jnp.where(even, pair_ref[part], next_ref[part])
        for k, cols in enumerate(parts):
            dst[k, 8:12, :] = before[:, cols]
            dst[k, 12:44, :] = own[:, cols]
            dst[k, 44:48, :] = after[:, cols]

    extend(coef_ref.at[0], cour_ref[...], 4)
    extend(coef_ref.at[1], diff_ref[...], 5)
    mid = slice(8, 48)
    for k in range(tiles):
        u, d = coef_ref[0, k, mid, :], coef_ref[1, k, mid, :]
        coef_ref[2, k, mid, :] = 1.0 - u - 4.0 * d
        coef_ref[0, k, mid, :] = u + d
    for c in range(4):
        extend(buf_ref.at[0, c], tot_ref[c], c)
    lane = lax.broadcasted_iota(jnp.int32, (40, LANES), 1)
    copies = []
    for step in range(STEPS):
        src, dst = step % 2, (step + 1) % 2
        for c in range(4):
            f = [buf_ref[src, c, k, mid, :] for k in range(tiles)]
            right = [pltpu.roll(v, 1, 1) for v in f]
            left = [pltpu.roll(v, LANES - 1, 1) for v in f]
            for k in range(tiles):
                west = jnp.where(lane == 0, right[k - 1] if k else 0.0, right[k])
                east = jnp.where(lane == LANES - 1, left[k + 1] if k + 1 < tiles else 0.0, left[k])
                up = buf_ref[src, c, k, 7:47, :]
                down = buf_ref[src, c, k, 9:49, :]
                new = coef_ref[2, k, mid, :] * f[k] + coef_ref[0, k, mid, :] * up
                new = new + coef_ref[1, k, mid, :] * (down + (west + east))
                buf_ref[dst, c, k, mid, :] = new
            if step == STEPS - 1:
                rows = slice(c * ROWS, (c + 1) * ROWS)
                for k in range(tiles):
                    res_ref[k, rows, :] = buf_ref[dst, c, k, 12:44, :]
                copies.append(pltpu.make_async_copy(res_ref.at[:, rows, :], out_ref.at[:, rows, :], sems.at[c]))
                copies[-1].start()
    for c in copies:
        c.wait()


def transport(pair, nxt, totals, courant, diffusion):
    tiles = totals.shape[2] // LANES
    return pl.pallas_call(
        transport_kernel,
        out_shape=jax.ShapeDtypeStruct((4, 4 * ROWS, LANES), jnp.float32),
        in_specs=[VMEM] * 5,
        out_specs=HBM,
        scratch_shapes=[
            pltpu.VMEM((2, 4, tiles, 56, LANES), jnp.float32),
            pltpu.VMEM((3, tiles, 56, LANES), jnp.float32),
            pltpu.VMEM((4, 4 * ROWS, LANES), jnp.float32),
            pltpu.SemaphoreType.DMA((4,)),
        ],
        compiler_params=pltpu.CompilerParams(vmem_limit_bytes=8 << 20),
        name="transport",
    )(*[on_chip(v) for v in (pair, nxt, totals, courant, diffusion)])


def tables_kernel(st_ref, ms_ref, lk_ref, mk_ref, mr_ref, counts_ref, flags_ref,
                  l1_ref, l2_ref, unit_ref, front_ref,
                  sq_ref, tab_ref, vec_ref, st, ms, lks, mks, mrs, cs, fs, sems):
    wide, narrow = lax.axis_index("wide"), lax.axis_index("narrow")
    copies = [pltpu.make_async_copy(src, dst, sems.at[n]) for n, (src, dst) in enumerate((
        (st_ref, st), (ms_ref, ms), (lk_ref, lks), (mk_ref, mks), (mr_ref, mrs), (counts_ref, cs), (flags_ref, fs)))]
    for c in copies:
        c.start()
    sq_ref[...] = jnp.zeros(sq_ref.shape, jnp.float32)
    vec_ref[...] = jnp.zeros(vec_ref.shape, jnp.float32)
    vec_ref[2:3, :] = jnp.ones((1, LANES), jnp.float32)
    for c in copies:
        c.wait()
    sq_ref[0, 0:NC, 0:NSEC] = st[...]
    sq_ref[1, NSEC:NSEC + NM, 0:NC] = ms[...]
    vec_ref[0:1, 0:NSEC] = lks[...]
    vec_ref[1:2, 0:NM] = mks[...]
    vec_ref[2:3, 0:NM] = mrs[...]
    at = sq_ref[0] + sq_ref[1].T
    vec = vec_ref[...]
    shifted = pltpu.roll(vec * -LOG2E, NSEC, 1)[1:2, :] + pltpu.roll(jnp.log(vec_ref[2:3, :]) * LOG2E, NSEC, 1)
    bias = vec[0:1, :] * LOG2E + shifted
    lane = lax.broadcasted_iota(jnp.int32, (1, LANES), 1)
    off = jnp.where((lane >= NSEC) & (lane < NSEC + NM), OFF, 0.0)
    hi, lo = split2(at[0:NC, :])
    b1, b2 = split2(bias)
    b3 = (bias - b1.astype(jnp.float32)) - b2.astype(jnp.float32)
    sq_ref[0, 0:NC, :] = hi.astype(jnp.float32)
    sq_ref[0, NC:2 * NC, :] = hi.astype(jnp.float32)
    sq_ref[0, 2 * NC:3 * NC, :] = lo.astype(jnp.float32)
    sq_ref[0, 48:49, :] = b1.astype(jnp.float32)
    sq_ref[0, 49:50, :] = b2.astype(jnp.float32)
    sq_ref[0, 50:51, :] = b3
    sq_ref[0, 51:52, :] = off
    l1_ref[...] = sq_ref[0].T[0:KS, 0:4 * NC].astype(jnp.bfloat16)
    row = 0
    for i in range(NC + 1):
        tab = at[i:NC, :] * at[i:i + 1, :] if i < NC else at[0:NC, :]
        n = tab.shape[0]
        tab_ref[row:row + n, :] = tab
        row += n
    hi, lo = split2(tab_ref[...])
    hi, lo = hi.astype(jnp.float32), lo.astype(jnp.float32)
    lo = pltpu.roll(lo, 2 * KS, 1)
    lane = lax.broadcasted_iota(jnp.int32, lo.shape, 1)
    l2_ref[:, 0:128] = jnp.where(lane < 2 * KS, hi + pltpu.roll(hi, KS, 1), lo).astype(jnp.bfloat16)
    l2_ref[:, 128:3 * KS] = lo[:, 0:3 * KS - 128].astype(jnp.bfloat16)
    row = lax.broadcasted_iota(jnp.int32, (16, LANES), 0)
    for b in range(NBLK):
        absent = 1.0 - fs[b].astype(jnp.float32)
        unit_ref[b] = jnp.where(row < 3, 1.0, jnp.where(row == 3, absent, 0.0)).astype(jnp.bfloat16)
    count = cs[narrow, wide]
    front_ref[...] = jnp.where(lax.broadcasted_iota(jnp.int32, (ROWS, LANES), 0) < 2 * count, 1.0, 0.0)


def tables(stoich, mineral_stoich, log_k, mineral_log_k, mineral_rate, counts, flags):
    return pl.pallas_call(
        tables_kernel,
        out_shape=[vmem_out((KS, 4 * NC), jnp.bfloat16), vmem_out((M2, 3 * KS), jnp.bfloat16),
                   vmem_out((NBLK, 16, LANES), jnp.bfloat16), vmem_out((ROWS, LANES))],
        in_specs=[HBM] * 7,
        out_specs=[VMEM] * 4,
        scratch_shapes=[
            pltpu.VMEM((2, 128, 128), jnp.float32), pltpu.VMEM((M2, 128), jnp.float32), pltpu.VMEM((8, LANES), jnp.float32),
            pltpu.VMEM((NC, NSEC), jnp.float32), pltpu.VMEM((NM, NC), jnp.float32),
            pltpu.VMEM((1, NSEC), jnp.float32), pltpu.VMEM((1, NM), jnp.float32), pltpu.VMEM((1, NM), jnp.float32),
            pltpu.SMEM(counts.shape, jnp.int32), pltpu.SMEM((NBLK,), jnp.int32),
            pltpu.SemaphoreType.DMA((7,)),
        ],
        compiler_params=pltpu.CompilerParams(vmem_limit_bytes=4 << 20),
        name="tables",
    )(*[in_hbm(v) for v in (stoich, mineral_stoich, log_k, mineral_log_k, mineral_rate, counts, flags)])


def speciate_kernel(l1_ref, l2_ref, unit_ref, front_ref, tot_ref, out_ref, y_ref, jac_ref, res_ref, sems):
    for k in range(NC):
        start = jnp.log(tot_ref[k * ROWS:(k + 1) * ROWS, :])
        res_ref[k] = start
        y_ref[k * PITCH:k * PITCH + ROWS, :] = start * LOG2E
    l1 = l1_ref[...]
    l2 = l2_ref[...]

    def stage(g):
        rows = range(8 * g, 8 * g + 8)
        ys = jnp.concatenate([y_ref[pl.ds(r, NC, stride=PITCH), :] for r in rows], axis=1)
        unit = jnp.concatenate([unit_ref[r // 2] for r in rows], axis=1)
        y1, y2 = split2(ys)
        s = jnp.dot(l1, jnp.concatenate([y1, y2, y1, unit], axis=0), preferred_element_type=jnp.float32)
        x1, x2 = split2(jnp.exp2(s))
        gm = jnp.dot(l2, jnp.concatenate([x1, x2, x1], axis=0), preferred_element_type=jnp.float32)
        for n, r in enumerate(rows):
            jac_ref[pl.ds(r, M2, stride=PITCH), :] = gm[:, n * LANES:(n + 1) * LANES]

    def solve(groups):
        def jac(p, g):
            return jac_ref[p * PITCH + 8 * g:p * PITCH + 8 * g + 8, :]

        def ysl(k, g):
            return slice(k * PITCH + 8 * g, k * PITCH + 8 * g + 8)

        w = {g: [[None] * NC for _ in range(NC + 1)] for g in groups}
        rd = {g: [None] * NC for g in groups}
        for j in range(NC):
            lj = {g: [w[g][j][k] * rd[g][k] for k in range(j)] for g in groups}
            for i in range(j, NC + 1):
                for g in groups:
                    if i == NC:
                        acc = jac(NP + j, g) + jnp.exp2(y_ref[ysl(j, g), :]) - tot_ref[j * ROWS + 8 * g:j * ROWS + 8 * g + 8, :]
                    else:
                        acc = jac(PIDX[(j, i)], g)
                        if i == j:
                            acc = acc + jnp.exp2(y_ref[ysl(j, g), :])
                    for k in range(j):
                        acc = acc - w[g][i][k] * lj[g][k]
                    w[g][i][j] = acc
                    if i == j:
                        rd[g][j] = 1.0 / acc
        sol = {g: [None] * NC for g in groups}
        for j in reversed(range(NC)):
            for g in groups:
                acc = w[g][NC][j]
                for i in reversed(range(j + 1, NC)):
                    acc = acc - w[g][i][j] * sol[g][i]
                sol[g][j] = acc * rd[g][j]
        for g in groups:
            largest = functools.reduce(jnp.maximum, [jnp.abs(v) for v in sol[g]])
            scale = LOG2E / jnp.maximum(largest, 1.0)
            for j in range(NC):
                y_ref[ysl(j, g), :] = y_ref[ysl(j, g), :] - sol[g][j] * scale

    copies = []

    def finish(half):
        rows = slice(16 * half, 16 * half + 16)
        front = front_ref[rows, :] > 0.5
        for k in range(NC):
            sol = y_ref[k * PITCH + 16 * half:k * PITCH + 16 * half + 16, :] * LN2
            res_ref[k, rows, :] = jnp.where(front, sol, res_ref[k, rows, :])
        copies.append(pltpu.make_async_copy(res_ref.at[:, rows, :], out_ref.at[:, rows, :], sems.at[half]))
        copies[-1].start()

    stage(0)
    stage(1)
    for it in range(ITERS):
        stage(2)
        stage(3)
        solve((0, 1))
        if it < ITERS - 1:
            stage(0)
            stage(1)
        else:
            finish(0)
        solve((2, 3))
    finish(1)
    for c in copies:
        c.wait()


def speciate(tabs, total):
    return pl.pallas_call(
        speciate_kernel,
        out_shape=jax.ShapeDtypeStruct((NC, ROWS, LANES), jnp.float32),
        in_specs=[VMEM] * 5,
        out_specs=HBM,
        scratch_shapes=[
            pltpu.VMEM((NC * PITCH, LANES), jnp.float32),
            pltpu.VMEM((M2 * PITCH, LANES), jnp.float32),
            pltpu.VMEM((NC, ROWS, LANES), jnp.float32),
            pltpu.SemaphoreType.DMA((2,)),
        ],
        compiler_params=pltpu.CompilerParams(vmem_limit_bytes=16 << 20),
        name="speciate",
    )(*[on_chip(v) for v in tabs], on_chip(total))


def shards(totals, courant, diffusion, stoich, log_k, mineral_stoich, mineral_log_k,
           mineral_rate, front_counts, mineral_flags):
    count = lax.axis_size("wide")
    pairs = [(i, i ^ 1) for i in range(count)]
    across = [(i, ((i + 1) ^ 1) - 1) for i in range(1, count - 1)]
    to_pair, to_next = pack(totals, courant, diffusion)
    pair = lax.ppermute(to_pair, "wide", pairs)
    nxt = lax.ppermute(to_next, "wide", across)
    moved = transport(pair, nxt, totals, courant, diffusion)
    total = lax.all_to_all(moved, "narrow", split_axis=0, concat_axis=0)
    tabs = tables(stoich.T, mineral_stoich, log_k.reshape(1, NSEC), mineral_log_k.reshape(1, NM), mineral_rate.reshape(1, NM),
                  front_counts.T, mineral_flags.reshape(NBLK))
    return speciate(tabs, total.reshape(NC * ROWS, LANES))


def solution(mesh):
    placed = (
        P("narrow", "wide", None), P("wide", None), P("wide", None),
        P(), P(), P(), P(), P(), P(), P("wide", "narrow"),
    )
    return jax.shard_map(
        shards, mesh=mesh, in_specs=placed, out_specs=P(None, "wide", "narrow"), check_vma=False
    )
```

time: 54.5 us -> 33.6 us (0.62)
  the two profiles are of different devices: /device:TPU:384 before, /device:TPU:1 now
where the time goes in v2:
time: 33.6 us; the launch traced here: 33.3 us
  starting transfers between devices  14.1 us (42%)
  Pallas kernels  11.3 us (34%)
  waiting for transfers between devices  7.82 us (23%)
    ppermute x1, starting transfers between devices, shards(): pair = lax.ppermute(to_pair, 'wide', pairs)  8.74 us
    pallas_call x1, Pallas kernels, speciate(): pl.pallas_call(speciate_kernel, out_shape=jax.ShapeDtypeStruct((NC, ROWS,...  7.66 us
    all_to_all x1, waiting for transfers between devices, shards(): total = lax.all_to_all(moved, 'narrow', split_axis=0, concat_axis=0)  4.35 us
    ppermute x1, waiting for transfers between devices, shards(): nxt = lax.ppermute(to_next, 'wide', across)  3.47 us
    all_to_all x1, starting transfers between devices, shards(): total = lax.all_to_all(moved, 'narrow', split_axis=0, concat_axis=0)  3.42 us
    ppermute x1, starting transfers between devices, shards(): nxt = lax.ppermute(to_next, 'wide', across)  1.92 us
    pallas_call x1, Pallas kernels, transport(): pl.pallas_call(transport_kernel, out_shape=jax.ShapeDtypeStruct((4, 4 * R...  1.51 us
    pallas_call x1, Pallas kernels, tables(): pl.pallas_call(tables_kernel, out_shape=[vmem_out((KS, 4 * NC), jnp.bfloa...  1.14 us
  transfers between devices with their start and end apart: 3, of which 2 were waited for; matrix products, arithmetic and copies ran while one was open for 0% of the time, Pallas kernels for 3%

profile of v2, /device:TPU:1, one launch (start us, length us, event | category | flops | bytes accessed | tf_op | source)
XLA Modules:
  0.0 33.3 jit_solution(2934946894798605811)
XLA Ops:
  0.0 0.0 copy-start.2
  0.0 0.0 copy-start.1
  0.0 0.0 copy-start
  0.0 1.0 %pack.1 = (f32[6,4,512]{2,1,0:T(4,128)S(1)}, f32[6,4,512]{2,1,0:T(4,128)S(1)}) custom-call(f32[4,32,512]{2,1,0:T(8,128)} %tot_ref.3, f32[32,512]{1,0:T(8,128)} %cour_ref.3, f32[32,512]{1,0:T(8,128)} %diff_ref.3), custom_call_target="tpu_custom_call" | custom-call | tf_op jit(solution)/shard_map/pack/pallas_call | solution.py:77
  1.1 8.7 %collective-permute-start = (f32[6,4,512]{2,1,0:T(4,128)S(1)}, f32[6,4,512]{2,1,0:T(4,128)S(1)}, u32[]{:S(2)}, u32[]{:S(2)}) collective-permute-start(f32[6,4,512]{2,1,0:T(4,128)S(1)} %get-tuple-element.15), channel_id=1, source_target_pairs={{0,4},{4,0},{8,12},{12,8},{16,20},{20,16},{24,28},{28,24},{32,36},... | collective-permute-start | bytes 147464 | tf_op jit(solution)/shard_map/ppermute | solution.py:341
  9.8 1.9 %collective-permute-start.1 = (f32[6,4,512]{2,1,0:T(4,128)S(1)}, f32[6,4,512]{2,1,0:T(4,128)S(1)}, u32[]{:S(2)}, u32[]{:S(2)}) collective-permute-start(f32[6,4,512]{2,1,0:T(4,128)S(1)} %get-tuple-element.16), channel_id=1, source_target_pairs={{4,8},{8,4},{12,16},{16,12},{20,24},{24,20},{28,32},{32,28},{36,40... | collective-permute-start | bytes 147464 | tf_op jit(solution)/shard_map/ppermute | solution.py:342
  11.7 0.0 collective-permute-done.pair_ref
  11.7 3.5 %collective-permute-done.1.next_ref = f32[6,4,512]{2,1,0:T(4,128)S(1)} collective-permute-done((f32[6,4,512]{2,1,0:T(4,128)S(1)}, f32[6,4,512]{2,1,0:T(4,128)S(1)}, u32[]{:S(2)}, u32[]{:S(2)}) %collective-permute-start.1) | collective-permute-done | bytes 49184 | tf_op jit(solution)/shard_map/ppermute | solution.py:342
  15.2 0.0 copy-done.2
  15.2 0.0 copy-done.1
  15.2 0.0 copy-done
  15.2 1.5 %transport.1 = f32[4,128,128]{2,1,0:T(8,128)} custom-call(f32[6,4,512]{2,1,0:T(4,128)S(1)} %collective-permute-done.pair_ref, f32[6,4,512]{2,1,0:T(4,128)S(1)} %collective-permute-done.1.next_ref, f32[4,32,512]{2,1,0:T(8,128)S(1)} %copy-done, f32[32,512]{1,0:T(8,128)S(1)} %copy-done.1, f32[32,512]{1,0:T(8,128)S(1)} %copy-done.2), custom_call_target="tpu_custom_call" | custom-call | tf_op jit(solution)/shard_map/transport/pallas_call | solution.py:144
  16.7 3.4 %all-to-all-start = ((f32[4,128,128]{2,1,0:T(8,128)}), f32[4,128,128]{2,1,0:T(8,128)S(1)}, u32[]{:S(2)}, u32[]{:S(2)}) async-start(f32[4,128,128]{2,1,0:T(8,128)} %transport.1), calls=%async_computation | async-start | bytes 524288 | tf_op jit(solution)/shard_map/all_to_all | solution.py:344
  20.2 1.1 %tables.1 = (bf16[48,64]{1,0:T(8,128)(2,1)S(1)}, bf16[152,144]{1,0:T(8,128)(2,1)S(1)}, bf16[16,16,128]{2,1,0:T(8,128)(2,1)S(1)}, f32[32,128]{1,0:T(8,128)S(1)}) custom-call(f32[16,32]{1,0:T(8,128)} %bitcast.8, f32[12,16]{1,0:T(8,128)} %ms_ref.1, f32[1,32]{1,0:T(1,128)} %bitcast.10, f32[1,12]{1,0:T(1,128)} %bitcast.11, f32[1,12]{1,0:T(1,128)} %bitcast.12, ...), custom_call_target="tpu_custom_call" | custom-call | tf_op jit(solution)/shard_map/tables/pallas_call | solution.py:216
  21.3 4.3 %all-to-all-done = f32[4,128,128]{2,1,0:T(8,128)S(1)} async-done(((f32[4,128,128]{2,1,0:T(8,128)}), f32[4,128,128]{2,1,0:T(8,128)S(1)}, u32[]{:S(2)}, u32[]{:S(2)}) %all-to-all-start) | async-done | bytes 262176 | tf_op jit(solution)/shard_map/all_to_all | solution.py:344
  25.7 7.7 %speciate.1 = f32[16,32,128]{2,1,0:T(8,128)} custom-call(bf16[48,64]{1,0:T(8,128)(2,1)S(1)} %get-tuple-element.11.l1_ref, bf16[152,144]{1,0:T(8,128)(2,1)S(1)} %get-tuple-element.12.l2_ref, bf16[16,16,128]{2,1,0:T(8,128)(2,1)S(1)} %get-tuple-element.13.unit_ref, f32[32,128]{1,0:T(8,128)S(1)} %get-tuple-element.14.front_ref, f32[512,128]{1,0:T(8,128)S(1)} %bitcast.7), custom_call_target="tpu_custom_call" | custom-call | tf_op jit(solution)/shard_map/speciate/pallas_call | solution.py:319
Async XLA Ops:
  0.0 15.2 %copy-start.2 = (f32[32,512]{1,0:T(8,128)S(1)}, f32[32,512]{1,0:T(8,128)}, u32[]{:S(2)}) copy-start(f32[32,512]{1,0:T(8,128)} %diff_ref.3) | copy-start | bytes 196612
  0.0 15.2 %copy-start.1 = (f32[32,512]{1,0:T(8,128)S(1)}, f32[32,512]{1,0:T(8,128)}, u32[]{:S(2)}) copy-start(f32[32,512]{1,0:T(8,128)} %cour_ref.3) | copy-start | bytes 196612
  0.0 15.2 %copy-start = (f32[4,32,512]{2,1,0:T(8,128)S(1)}, f32[4,32,512]{2,1,0:T(8,128)}, u32[]{:S(2)}) copy-start(f32[4,32,512]{2,1,0:T(8,128)} %tot_ref.3) | copy-start | bytes 786436
  1.1 10.7 %collective-permute-start = (f32[6,4,512]{2,1,0:T(4,128)S(1)}, f32[6,4,512]{2,1,0:T(4,128)S(1)}, u32[]{:S(2)}, u32[]{:S(2)}) collective-permute-start(f32[6,4,512]{2,1,0:T(4,128)S(1)} %get-tuple-element.15), channel_id=1, source_target_pairs={{0,4},{4,0},{8,12},{12,8},{16,20},{20,16},{24,28},{28,24},{32,36},... | collective-permute-start | bytes 147464 | tf_op jit(solution)/shard_map/ppermute | solution.py:341
  9.8 5.4 %collective-permute-start.1 = (f32[6,4,512]{2,1,0:T(4,128)S(1)}, f32[6,4,512]{2,1,0:T(4,128)S(1)}, u32[]{:S(2)}, u32[]{:S(2)}) collective-permute-start(f32[6,4,512]{2,1,0:T(4,128)S(1)} %get-tuple-element.16), channel_id=1, source_target_pairs={{4,8},{8,4},{12,16},{16,12},{20,24},{24,20},{28,32},{32,28},{36,40... | collective-permute-start | bytes 147464 | tf_op jit(solution)/shard_map/ppermute | solution.py:342
  16.7 8.9 %all-to-all-start = ((f32[4,128,128]{2,1,0:T(8,128)}), f32[4,128,128]{2,1,0:T(8,128)S(1)}, u32[]{:S(2)}, u32[]{:S(2)}) async-start(f32[4,128,128]{2,1,0:T(8,128)} %transport.1), calls=%async_computation | async-start | bytes 524288 | tf_op jit(solution)/shard_map/all_to_all | solution.py:344

commit v3 on v2

--- a/solution.py
+++ b/solution.py
@@ -7,10 +7,11 @@
 from jax.experimental.pallas import tpu as pltpu
 from jax.sharding import PartitionSpec as P
 
+
 STEPS = 4
 ITERS = 4
 HALO = 4
-CHUNK = 8
+EARLY, LATE = 4, 2
 NC = 16
 ROWS = 32
 LANES = 128
@@ -113,28 +114,36 @@
         coef_ref[0, k, mid, :] = u + d
     for c in range(4):
         extend(buf_ref.at[0, c], tot_ref[c], c)
-    lane = lax.broadcasted_iota(jnp.int32, (40, LANES), 1)
     copies = []
+
+    def advance(step, c):
+        src, dst = step % 2, (step + 1) % 2
+        last = step == STEPS - 1
+        lo, hi = (12, 44) if last else (8, 48)
+        rows = slice(lo, hi)
+        lane = lax.broadcasted_iota(jnp.int32, (hi - lo, LANES), 1)
+        f = [buf_ref[src, c, k, rows, :] for k in range(tiles)]
+        right = [pltpu.roll(v, 1, 1) for v in f]
+        left = [pltpu.roll(v, LANES - 1, 1) for v in f]
+        for k in range(tiles):
+            west = jnp.where(lane == 0, right[k - 1] if k else 0.0, right[k])
+            east = jnp.where(lane == LANES - 1, left[k + 1] if k + 1 < tiles else 0.0, left[k])
+            up = buf_ref[src, c, k, lo - 1:hi - 1, :]
+            down = buf_ref[src, c, k, lo + 1:hi + 1, :]
+            new = coef_ref[2, k, rows, :] * f[k] + coef_ref[0, k, rows, :] * up
+            new = new + coef_ref[1, k, rows, :] * (down + (west + east))
+            if last:
+                res_ref[k, c * ROWS:(c + 1) * ROWS, :] = new
+            else:
+                buf_ref[dst, c, k, rows, :] = new
+        if last:
+            own = slice(c * ROWS, (c + 1) * ROWS)
+            copies.append(pltpu.make_async_copy(res_ref.at[:, own, :], out_ref.at[:, own, :], sems.at[c]))
+            copies[-1].start()
+
     for step in range(STEPS):
-        src, dst = step % 2, (step + 1) % 2
         for c in range(4):
-            f = [buf_ref[src, c, k, mid, :] for k in range(tiles)]
-            right = [pltpu.roll(v, 1, 1) for v in f]
-            left = [pltpu.roll(v, LANES - 1, 1) for v in f]
-            for k in range(tiles):
-                west = jnp.where(lane == 0, right[k - 1] if k else 0.0, right[k])
-                east = jnp.where(lane == LANES - 1, left[k + 1] if k + 1 < tiles else 0.0, left[k])
-                up = buf_ref[src, c, k, 7:47, :]
-                down = buf_ref[src, c, k, 9:49, :]
-                new = coef_ref[2, k, mid, :] * f[k] + coef_ref[0, k, mid, :] * up
-                new = new + coef_ref[1, k, mid, :] * (down + (west + east))
-                buf_ref[dst, c, k, mid, :] = new
-            if step == STEPS - 1:
-                rows = slice(c * ROWS, (c + 1) * ROWS)
-                for k in range(tiles):
-                    res_ref[k, rows, :] = buf_ref[dst, c, k, 12:44, :]
-                copies.append(pltpu.make_async_copy(res_ref.at[:, rows, :], out_ref.at[:, rows, :], sems.at[c]))
-                copies[-1].start()
+            advance(step, c)
     for c in copies:
         c.wait()
 
@@ -239,16 +248,23 @@
     l1 = l1_ref[...]
     l2 = l2_ref[...]
 
-    def stage(g):
-        rows = range(8 * g, 8 * g + 8)
-        ys = jnp.concatenate([y_ref[pl.ds(r, NC, stride=PITCH), :] for r in rows], axis=1)
-        unit = jnp.concatenate([unit_ref[r // 2] for r in rows], axis=1)
-        y1, y2 = split2(ys)
-        s = jnp.dot(l1, jnp.concatenate([y1, y2, y1, unit], axis=0), preferred_element_type=jnp.float32)
-        x1, x2 = split2(jnp.exp2(s))
-        gm = jnp.dot(l2, jnp.concatenate([x1, x2, x1], axis=0), preferred_element_type=jnp.float32)
-        for n, r in enumerate(rows):
-            jac_ref[pl.ds(r, M2, stride=PITCH), :] = gm[:, n * LANES:(n + 1) * LANES]
+    def stage(groups):
+        s, x = {}, {}
+        for g in groups:
+            rows = range(8 * g, 8 * g + 8)
+            ys = jnp.concatenate([y_ref[pl.ds(r, NC, stride=PITCH), :] for r in rows], axis=1)
+            unit = jnp.concatenate([unit_ref[r // 2] for r in rows], axis=1)
+            y1, y2 = split2(ys)
+            s[g] = jnp.dot(l1, jnp.concatenate([y1, y2, y1, unit], axis=0), preferred_element_type=jnp.float32)
+            yield
+        for g in groups:
+            x1, x2 = split2(jnp.exp2(s[g]))
+            x[g] = jnp.concatenate([x1, x2, x1], axis=0)
+            yield
+            gm = jnp.dot(l2, x[g], preferred_element_type=jnp.float32)
+            for n in range(8):
+                jac_ref[pl.ds(8 * g + n, M2, stride=PITCH), :] = gm[:, n * LANES:(n + 1) * LANES]
+            yield
 
     def solve(groups):
         def jac(p, g):
@@ -274,6 +290,7 @@
                     w[g][i][j] = acc
                     if i == j:
                         rd[g][j] = 1.0 / acc
+            yield
         sol = {g: [None] * NC for g in groups}
         for j in reversed(range(NC)):
             for g in groups:
@@ -281,13 +298,17 @@
                 for i in reversed(range(j + 1, NC)):
                     acc = acc - w[g][i][j] * sol[g][i]
                 sol[g][j] = acc * rd[g][j]
+            yield
         for g in groups:
             largest = functools.reduce(jnp.maximum, [jnp.abs(v) for v in sol[g]])
             scale = LOG2E / jnp.maximum(largest, 1.0)
             for j in range(NC):
                 y_ref[ysl(j, g), :] = y_ref[ysl(j, g), :] - sol[g][j] * scale
-
-    copies = []
+        yield
+
+    def out_copy(half):
+        rows = slice(16 * half, 16 * half + 16)
+        return pltpu.make_async_copy(res_ref.at[:, rows, :], out_ref.at[:, rows, :], sems.at[half])
 
     def finish(half):
         rows = slice(16 * half, 16 * half + 16)
@@ -295,24 +316,49 @@
         for k in range(NC):
             sol = y_ref[k * PITCH + 16 * half:k * PITCH + 16 * half + 16, :] * LN2
             res_ref[k, rows, :] = jnp.where(front, sol, res_ref[k, rows, :])
-        copies.append(pltpu.make_async_copy(res_ref.at[:, rows, :], out_ref.at[:, rows, :], sems.at[half]))
-        copies[-1].start()
-
-    stage(0)
-    stage(1)
-    for it in range(ITERS):
-        stage(2)
-        stage(3)
-        solve((0, 1))
-        if it < ITERS - 1:
-            stage(0)
-            stage(1)
-        else:
-            finish(0)
-        solve((2, 3))
-    finish(1)
-    for c in copies:
-        c.wait()
+        out_copy(half).start()
+
+    def weave(*plans):
+        slots = sorted((step / count, n) for n, (_, count) in enumerate(plans) for step in range(count))
+        for _, n in slots:
+            next(plans[n][0])
+
+    halves = ((0, 1), (2, 3))
+    pieces = 6
+    both = front_ref[16, 0] > 0.5
+
+    @pl.when(both)
+    def _():
+        weave((stage(halves[0]), pieces))
+        now = solve(halves[0])
+        weave((now, EARLY))
+        for turn in range(2 * ITERS):
+            half = turn % 2
+            other = None
+            if turn + 1 < 2 * ITERS:
+                weave((now, NC - EARLY - LATE), (stage(halves[1 - half]), pieces))
+                other = solve(halves[1 - half])
+                weave((now, LATE + NC + 1), (other, EARLY))
+            else:
+                weave((now, NC - EARLY + NC + 1))
+            if turn >= 2 * ITERS - 2:
+                finish(half)
+            now = other
+
+    @pl.when(jnp.logical_not(both))
+    def _():
+        out_copy(1).start()
+
+        def body(it, carry):
+            weave((stage(halves[0]), pieces))
+            weave((solve(halves[0]), 2 * NC + 1))
+            return carry
+
+        lax.fori_loop(0, ITERS, body, 0)
+        finish(0)
+
+    out_copy(0).wait()
+    out_copy(1).wait()
 
 
 def speciate(tabs, total):
@@ -338,8 +384,8 @@
     pairs = [(i, i ^ 1) for i in range(count)]
     across = [(i, ((i + 1) ^ 1) - 1) for i in range(1, count - 1)]
     to_pair, to_next = pack(totals, courant, diffusion)
+    nxt = lax.ppermute(to_next, "wide", across)
     pair = lax.ppermute(to_pair, "wide", pairs)
-    nxt = lax.ppermute(to_next, "wide", across)
     moved = transport(pair, nxt, totals, courant, diffusion)
     total = lax.all_to_all(moved, "narrow", split_axis=0, concat_axis=0)
     tabs = tables(stoich.T, mineral_stoich, log_k.reshape(1, NSEC), mineral_log_k.reshape(1, NM), mineral_rate.reshape(1, NM),

time: 33.6 us -> 32 us (0.952)
  the two profiles are of different devices: /device:TPU:1 before, /device:TPU:2 now
where the time goes in v3:
time: 32 us; the launch traced here: 31.7 us
  starting transfers between devices  13.2 us (41%)
  Pallas kernels  11.2 us (35%)
  waiting for transfers between devices  7.25 us (23%)
    ppermute x1, starting transfers between devices, shards(): nxt = lax.ppermute(to_next, 'wide', across)  7.89 us
    pallas_call x1, Pallas kernels, speciate(): pl.pallas_call(speciate_kernel, out_shape=jax.ShapeDtypeStruct((NC, ROWS,...  7.52 us
    all_to_all x1, waiting for transfers between devices, shards(): total = lax.all_to_all(moved, 'narrow', split_axis=0, concat_axis=0)  5.5 us
    all_to_all x1, starting transfers between devices, shards(): total = lax.all_to_all(moved, 'narrow', split_axis=0, concat_axis=0)  3.42 us
    ppermute x1, starting transfers between devices, shards(): pair = lax.ppermute(to_pair, 'wide', pairs)  1.92 us
    ppermute x1, waiting for transfers between devices, shards(): nxt = lax.ppermute(to_next, 'wide', across)  1.75 us
    pallas_call x1, Pallas kernels, transport(): pl.pallas_call(transport_kernel, out_shape=jax.ShapeDtypeStruct((4, 4 * R...  1.46 us
    pallas_call x1, Pallas kernels, tables(): pl.pallas_call(tables_kernel, out_shape=[vmem_out((KS, 4 * NC), jnp.bfloa...  1.14 us
  transfers between devices with their start and end apart: 3, of which 2 were waited for; matrix products, arithmetic and copies ran while one was open for 0% of the time, Pallas kernels for 4%

profile of v3, /device:TPU:2, one launch (start us, length us, event | category | flops | bytes accessed | tf_op | source)
XLA Modules:
  0.0 31.7 jit_solution(3598197000767360868)
XLA Ops:
  0.0 0.0 copy-start.2
  0.0 0.0 copy-start.1
  0.0 0.0 copy-start
  0.0 1.0 %pack.1 = (f32[6,4,512]{2,1,0:T(4,128)S(1)}, f32[6,4,512]{2,1,0:T(4,128)S(1)}) custom-call(f32[4,32,512]{2,1,0:T(8,128)} %tot_ref.3, f32[32,512]{1,0:T(8,128)} %cour_ref.3, f32[32,512]{1,0:T(8,128)} %diff_ref.3), custom_call_target="tpu_custom_call" | custom-call | tf_op jit(solution)/shard_map/pack/pallas_call | solution.py:78
  1.1 1.9 %collective-permute-start = (f32[6,4,512]{2,1,0:T(4,128)S(1)}, f32[6,4,512]{2,1,0:T(4,128)S(1)}, u32[]{:S(2)}, u32[]{:S(2)}) collective-permute-start(f32[6,4,512]{2,1,0:T(4,128)S(1)} %get-tuple-element.15), channel_id=1, source_target_pairs={{0,4},{4,0},{8,12},{12,8},{16,20},{20,16},{24,28},{28,24},{32,36},... | collective-permute-start | bytes 147464 | tf_op jit(solution)/shard_map/ppermute | solution.py:388
  3.0 7.9 %collective-permute-start.1 = (f32[6,4,512]{2,1,0:T(4,128)S(1)}, f32[6,4,512]{2,1,0:T(4,128)S(1)}, u32[]{:S(2)}, u32[]{:S(2)}) collective-permute-start(f32[6,4,512]{2,1,0:T(4,128)S(1)} %get-tuple-element.16), channel_id=1, source_target_pairs={{4,8},{8,4},{12,16},{16,12},{20,24},{24,20},{28,32},{32,28},{36,40... | collective-permute-start | bytes 147464 | tf_op jit(solution)/shard_map/ppermute | solution.py:387
  10.9 0.0 collective-permute-done.pair_ref
  10.9 1.7 %collective-permute-done.1.next_ref = f32[6,4,512]{2,1,0:T(4,128)S(1)} collective-permute-done((f32[6,4,512]{2,1,0:T(4,128)S(1)}, f32[6,4,512]{2,1,0:T(4,128)S(1)}, u32[]{:S(2)}, u32[]{:S(2)}) %collective-permute-start.1) | collective-permute-done | bytes 49184 | tf_op jit(solution)/shard_map/ppermute | solution.py:387
  12.6 0.0 copy-done.2
  12.6 0.0 copy-done.1
  12.6 0.0 copy-done
  12.6 1.5 %transport.1 = f32[4,128,128]{2,1,0:T(8,128)} custom-call(f32[6,4,512]{2,1,0:T(4,128)S(1)} %collective-permute-done.pair_ref, f32[6,4,512]{2,1,0:T(4,128)S(1)} %collective-permute-done.1.next_ref, f32[4,32,512]{2,1,0:T(8,128)S(1)} %copy-done, f32[32,512]{1,0:T(8,128)S(1)} %copy-done.1, f32[32,512]{1,0:T(8,128)S(1)} %copy-done.2), custom_call_target="tpu_custom_call" | custom-call | tf_op jit(solution)/shard_map/transport/pallas_call | solution.py:153
  14.1 3.4 %all-to-all-start = ((f32[4,128,128]{2,1,0:T(8,128)}), f32[4,128,128]{2,1,0:T(8,128)S(1)}, u32[]{:S(2)}, u32[]{:S(2)}) async-start(f32[4,128,128]{2,1,0:T(8,128)} %transport.1), calls=%async_computation | async-start | bytes 524288 | tf_op jit(solution)/shard_map/all_to_all | solution.py:390
  17.5 1.1 %tables.1 = (bf16[48,64]{1,0:T(8,128)(2,1)S(1)}, bf16[152,144]{1,0:T(8,128)(2,1)S(1)}, bf16[16,16,128]{2,1,0:T(8,128)(2,1)S(1)}, f32[32,128]{1,0:T(8,128)S(1)}) custom-call(f32[16,32]{1,0:T(8,128)} %bitcast.8, f32[12,16]{1,0:T(8,128)} %ms_ref.1, f32[1,32]{1,0:T(1,128)} %bitcast.10, f32[1,12]{1,0:T(1,128)} %bitcast.11, f32[1,12]{1,0:T(1,128)} %bitcast.12, ...), custom_call_target="tpu_custom_call" | custom-call | tf_op jit(solution)/shard_map/tables/pallas_call | solution.py:225
  18.7 5.5 %all-to-all-done = f32[4,128,128]{2,1,0:T(8,128)S(1)} async-done(((f32[4,128,128]{2,1,0:T(8,128)}), f32[4,128,128]{2,1,0:T(8,128)S(1)}, u32[]{:S(2)}, u32[]{:S(2)}) %all-to-all-start) | async-done | bytes 262176 | tf_op jit(solution)/shard_map/all_to_all | solution.py:390
  24.2 7.5 %speciate.1 = f32[16,32,128]{2,1,0:T(8,128)} custom-call(bf16[48,64]{1,0:T(8,128)(2,1)S(1)} %get-tuple-element.11.l1_ref, bf16[152,144]{1,0:T(8,128)(2,1)S(1)} %get-tuple-element.12.l2_ref, bf16[16,16,128]{2,1,0:T(8,128)(2,1)S(1)} %get-tuple-element.13.unit_ref, f32[32,128]{1,0:T(8,128)S(1)} %get-tuple-element.14.front_ref, f32[512,128]{1,0:T(8,128)S(1)} %bitcast.7), custom_call_target="tpu_custom_call" | custom-call | tf_op jit(solution)/shard_map/speciate/pallas_call | solution.py:365
Async XLA Ops:
  0.0 12.6 %copy-start.2 = (f32[32,512]{1,0:T(8,128)S(1)}, f32[32,512]{1,0:T(8,128)}, u32[]{:S(2)}) copy-start(f32[32,512]{1,0:T(8,128)} %diff_ref.3) | copy-start | bytes 196612
  0.0 12.6 %copy-start.1 = (f32[32,512]{1,0:T(8,128)S(1)}, f32[32,512]{1,0:T(8,128)}, u32[]{:S(2)}) copy-start(f32[32,512]{1,0:T(8,128)} %cour_ref.3) | copy-start | bytes 196612
  0.0 12.6 %copy-start = (f32[4,32,512]{2,1,0:T(8,128)S(1)}, f32[4,32,512]{2,1,0:T(8,128)}, u32[]{:S(2)}) copy-start(f32[4,32,512]{2,1,0:T(8,128)} %tot_ref.3) | copy-start | bytes 786436
  1.1 9.8 %collective-permute-start = (f32[6,4,512]{2,1,0:T(4,128)S(1)}, f32[6,4,512]{2,1,0:T(4,128)S(1)}, u32[]{:S(2)}, u32[]{:S(2)}) collective-permute-start(f32[6,4,512]{2,1,0:T(4,128)S(1)} %get-tuple-element.15), channel_id=1, source_target_pairs={{0,4},{4,0},{8,12},{12,8},{16,20},{20,16},{24,28},{28,24},{32,36},... | collective-permute-start | bytes 147464 | tf_op jit(solution)/shard_map/ppermute | solution.py:388
  3.0 9.7 %collective-permute-start.1 = (f32[6,4,512]{2,1,0:T(4,128)S(1)}, f32[6,4,512]{2,1,0:T(4,128)S(1)}, u32[]{:S(2)}, u32[]{:S(2)}) collective-permute-start(f32[6,4,512]{2,1,0:T(4,128)S(1)} %get-tuple-element.16), channel_id=1, source_target_pairs={{4,8},{8,4},{12,16},{16,12},{20,24},{24,20},{28,32},{32,28},{36,40... | collective-permute-start | bytes 147464 | tf_op jit(solution)/shard_map/ppermute | solution.py:387
  14.1 10.1 %all-to-all-start = ((f32[4,128,128]{2,1,0:T(8,128)}), f32[4,128,128]{2,1,0:T(8,128)S(1)}, u32[]{:S(2)}, u32[]{:S(2)}) async-start(f32[4,128,128]{2,1,0:T(8,128)} %transport.1), calls=%async_computation | async-start | bytes 524288 | tf_op jit(solution)/shard_map/all_to_all | solution.py:390

commit v4 on v3

--- a/solution.py
+++ b/solution.py
@@ -20,7 +20,7 @@
 NM = 12
 KS = 48
 OFF = -16384.0
-PITCH = 33
+PITCH = 9
 LOG2E = 1.4426950408889634
 LN2 = 0.6931471805599453
 PAIRS = [(i, j) for i in range(NC) for j in range(i, NC)]
@@ -240,11 +240,13 @@
     )(*[in_hbm(v) for v in (stoich, mineral_stoich, log_k, mineral_log_k, mineral_rate, counts, flags)])
 
 
-def speciate_kernel(l1_ref, l2_ref, unit_ref, front_ref, tot_ref, out_ref, y_ref, jac_ref, res_ref, sems):
+def speciate_kernel(l1_ref, l2_ref, unit_ref, front_ref, tot_ref, out_ref, res_ref, sems, *scratch):
+    y_refs, jac_refs = scratch[:4], scratch[4:]
     for k in range(NC):
         start = jnp.log(tot_ref[k * ROWS:(k + 1) * ROWS, :])
         res_ref[k] = start
-        y_ref[k * PITCH:k * PITCH + ROWS, :] = start * LOG2E
+        for g, y_ref in enumerate(y_refs):
+            y_ref[k * PITCH:k * PITCH + 8, :] = start[8 * g:8 * g + 8] * LOG2E
     l1 = l1_ref[...]
     l2 = l2_ref[...]
 
@@ -252,7 +254,7 @@
         s, x = {}, {}
         for g in groups:
             rows = range(8 * g, 8 * g + 8)
-            ys = jnp.concatenate([y_ref[pl.ds(r, NC, stride=PITCH), :] for r in rows], axis=1)
+            ys = jnp.concatenate([y_refs[g][pl.ds(r, NC, stride=PITCH), :] for r in range(8)], axis=1)
             unit = jnp.concatenate([unit_ref[r // 2] for r in rows], axis=1)
             y1, y2 = split2(ys)
             s[g] = jnp.dot(l1, jnp.concatenate([y1, y2, y1, unit], axis=0), preferred_element_type=jnp.float32)
@@ -263,15 +265,15 @@
             yield
             gm = jnp.dot(l2, x[g], preferred_element_type=jnp.float32)
             for n in range(8):
-                jac_ref[pl.ds(8 * g + n, M2, stride=PITCH), :] = gm[:, n * LANES:(n + 1) * LANES]
+                jac_refs[g][pl.ds(n, M2, stride=PITCH), :] = gm[:, n * LANES:(n + 1) * LANES]
             yield
 
     def solve(groups):
         def jac(p, g):
-            return jac_ref[p * PITCH + 8 * g:p * PITCH + 8 * g + 8, :]
-
-        def ysl(k, g):
-            return slice(k * PITCH + 8 * g, k * PITCH + 8 * g + 8)
+            return jac_refs[g][p * PITCH:p * PITCH + 8, :]
+
+        def ysl(k):
+            return slice(k * PITCH, k * PITCH + 8)
 
         w = {g: [[None] * NC for _ in range(NC + 1)] for g in groups}
         rd = {g: [None] * NC for g in groups}
@@ -280,11 +282,11 @@
             for i in range(j, NC + 1):
                 for g in groups:
                     if i == NC:
-                        acc = jac(NP + j, g) + jnp.exp2(y_ref[ysl(j, g), :]) - tot_ref[j * ROWS + 8 * g:j * ROWS + 8 * g + 8, :]
+                        acc = jac(NP + j, g) + jnp.exp2(y_refs[g][ysl(j), :]) - tot_ref[j * ROWS + 8 * g:j * ROWS + 8 * g + 8, :]
                     else:
                         acc = jac(PIDX[(j, i)], g)
                         if i == j:
-                            acc = acc + jnp.exp2(y_ref[ysl(j, g), :])
+                            acc = acc + jnp.exp2(y_refs[g][ysl(j), :])
                     for k in range(j):
                         acc = acc - w[g][i][k] * lj[g][k]
                     w[g][i][j] = acc
@@ -303,7 +305,7 @@
             largest = functools.reduce(jnp.maximum, [jnp.abs(v) for v in sol[g]])
             scale = LOG2E / jnp.maximum(largest, 1.0)
             for j in range(NC):
-                y_ref[ysl(j, g), :] = y_ref[ysl(j, g), :] - sol[g][j] * scale
+                y_refs[g][ysl(j), :] = y_refs[g][ysl(j), :] - sol[g][j] * scale
         yield
 
     def out_copy(half):
@@ -314,7 +316,7 @@
         rows = slice(16 * half, 16 * half + 16)
         front = front_ref[rows, :] > 0.5
         for k in range(NC):
-            sol = y_ref[k * PITCH + 16 * half:k * PITCH + 16 * half + 16, :] * LN2
+            sol = jnp.concatenate([y_refs[g][k * PITCH:k * PITCH + 8, :] for g in halves[half]], axis=0) * LN2
             res_ref[k, rows, :] = jnp.where(front, sol, res_ref[k, rows, :])
         out_copy(half).start()
 
@@ -368,10 +370,10 @@
         in_specs=[VMEM] * 5,
         out_specs=HBM,
         scratch_shapes=[
-            pltpu.VMEM((NC * PITCH, LANES), jnp.float32),
-            pltpu.VMEM((M2 * PITCH, LANES), jnp.float32),
             pltpu.VMEM((NC, ROWS, LANES), jnp.float32),
             pltpu.SemaphoreType.DMA((2,)),
+            *[pltpu.VMEM((NC * PITCH, LANES), jnp.float32)] * 4,
+            *[pltpu.VMEM((M2 * PITCH, LANES), jnp.float32)] * 4,
         ],
         compiler_params=pltpu.CompilerParams(vmem_limit_bytes=16 << 20),
         name="speciate",

time: 32 us -> 31.9 us (level)
  no operation moved by 1% of the time
where the time goes in v4:
time: 31.9 us; the launch traced here: 31.7 us
  starting transfers between devices  13.2 us (41%)
  Pallas kernels  11.1 us (35%)
  waiting for transfers between devices  7.25 us (23%)
    ppermute x1, starting transfers between devices, shards(): nxt = lax.ppermute(to_next, 'wide', across)  7.89 us
    pallas_call x1, Pallas kernels, speciate(): pl.pallas_call(speciate_kernel, out_shape=jax.ShapeDtypeStruct((NC, ROWS,...  7.47 us
    all_to_all x1, waiting for transfers between devices, shards(): total = lax.all_to_all(moved, 'narrow', split_axis=0, concat_axis=0)  5.5 us
    all_to_all x1, starting transfers between devices, shards(): total = lax.all_to_all(moved, 'narrow', split_axis=0, concat_axis=0)  3.42 us
    ppermute x1, starting transfers between devices, shards(): pair = lax.ppermute(to_pair, 'wide', pairs)  1.92 us
    ppermute x1, waiting for transfers between devices, shards(): nxt = lax.ppermute(to_next, 'wide', across)  1.75 us
    pallas_call x1, Pallas kernels, transport(): pl.pallas_call(transport_kernel, out_shape=jax.ShapeDtypeStruct((4, 4 * R...  1.46 us
    pallas_call x1, Pallas kernels, tables(): pl.pallas_call(tables_kernel, out_shape=[vmem_out((KS, 4 * NC), jnp.bfloa...  1.14 us
  transfers between devices with their start and end apart: 3, of which 2 were waited for; matrix products, arithmetic and copies ran while one was open for 0% of the time, Pallas kernels for 4%

profile of v4, /device:TPU:2, one launch (start us, length us, event | category | flops | bytes accessed | tf_op | source)
XLA Modules:
  0.0 31.7 jit_solution(1410541309559312656)
XLA Ops:
  0.0 0.0 copy-start.2
  0.0 0.0 copy-start.1
  0.0 0.0 copy-start
  0.0 1.0 %pack.1 = (f32[6,4,512]{2,1,0:T(4,128)S(1)}, f32[6,4,512]{2,1,0:T(4,128)S(1)}) custom-call(f32[4,32,512]{2,1,0:T(8,128)} %tot_ref.3, f32[32,512]{1,0:T(8,128)} %cour_ref.3, f32[32,512]{1,0:T(8,128)} %diff_ref.3), custom_call_target="tpu_custom_call" | custom-call | tf_op jit(solution)/shard_map/pack/pallas_call | solution.py:78
  1.1 1.9 %collective-permute-start = (f32[6,4,512]{2,1,0:T(4,128)S(1)}, f32[6,4,512]{2,1,0:T(4,128)S(1)}, u32[]{:S(2)}, u32[]{:S(2)}) collective-permute-start(f32[6,4,512]{2,1,0:T(4,128)S(1)} %get-tuple-element.15), channel_id=1, source_target_pairs={{0,4},{4,0},{8,12},{12,8},{16,20},{20,16},{24,28},{28,24},{32,36},... | collective-permute-start | bytes 147464 | tf_op jit(solution)/shard_map/ppermute | solution.py:390
  3.0 7.9 %collective-permute-start.1 = (f32[6,4,512]{2,1,0:T(4,128)S(1)}, f32[6,4,512]{2,1,0:T(4,128)S(1)}, u32[]{:S(2)}, u32[]{:S(2)}) collective-permute-start(f32[6,4,512]{2,1,0:T(4,128)S(1)} %get-tuple-element.16), channel_id=1, source_target_pairs={{4,8},{8,4},{12,16},{16,12},{20,24},{24,20},{28,32},{32,28},{36,40... | collective-permute-start | bytes 147464 | tf_op jit(solution)/shard_map/ppermute | solution.py:389
  10.9 0.0 collective-permute-done.pair_ref
  10.9 1.7 %collective-permute-done.1.next_ref = f32[6,4,512]{2,1,0:T(4,128)S(1)} collective-permute-done((f32[6,4,512]{2,1,0:T(4,128)S(1)}, f32[6,4,512]{2,1,0:T(4,128)S(1)}, u32[]{:S(2)}, u32[]{:S(2)}) %collective-permute-start.1) | collective-permute-done | bytes 49184 | tf_op jit(solution)/shard_map/ppermute | solution.py:389
  12.6 0.0 copy-done.2
  12.6 0.0 copy-done.1
  12.6 0.0 copy-done
  12.6 1.5 %transport.1 = f32[4,128,128]{2,1,0:T(8,128)} custom-call(f32[6,4,512]{2,1,0:T(4,128)S(1)} %collective-permute-done.pair_ref, f32[6,4,512]{2,1,0:T(4,128)S(1)} %collective-permute-done.1.next_ref, f32[4,32,512]{2,1,0:T(8,128)S(1)} %copy-done, f32[32,512]{1,0:T(8,128)S(1)} %copy-done.1, f32[32,512]{1,0:T(8,128)S(1)} %copy-done.2), custom_call_target="tpu_custom_call" | custom-call | tf_op jit(solution)/shard_map/transport/pallas_call | solution.py:153
  14.1 3.4 %all-to-all-start = ((f32[4,128,128]{2,1,0:T(8,128)}), f32[4,128,128]{2,1,0:T(8,128)S(1)}, u32[]{:S(2)}, u32[]{:S(2)}) async-start(f32[4,128,128]{2,1,0:T(8,128)} %transport.1), calls=%async_computation | async-start | bytes 524288 | tf_op jit(solution)/shard_map/all_to_all | solution.py:392
  17.5 1.1 %tables.1 = (bf16[48,64]{1,0:T(8,128)(2,1)S(1)}, bf16[152,144]{1,0:T(8,128)(2,1)S(1)}, bf16[16,16,128]{2,1,0:T(8,128)(2,1)S(1)}, f32[32,128]{1,0:T(8,128)S(1)}) custom-call(f32[16,32]{1,0:T(8,128)} %bitcast.8, f32[12,16]{1,0:T(8,128)} %ms_ref.1, f32[1,32]{1,0:T(1,128)} %bitcast.10, f32[1,12]{1,0:T(1,128)} %bitcast.11, f32[1,12]{1,0:T(1,128)} %bitcast.12, ...), custom_call_target="tpu_custom_call" | custom-call | tf_op jit(solution)/shard_map/tables/pallas_call | solution.py:225
  18.7 5.5 %all-to-all-done = f32[4,128,128]{2,1,0:T(8,128)S(1)} async-done(((f32[4,128,128]{2,1,0:T(8,128)}), f32[4,128,128]{2,1,0:T(8,128)S(1)}, u32[]{:S(2)}, u32[]{:S(2)}) %all-to-all-start) | async-done | bytes 262176 | tf_op jit(solution)/shard_map/all_to_all | solution.py:392
  24.2 7.5 %speciate.1 = f32[16,32,128]{2,1,0:T(8,128)} custom-call(bf16[48,64]{1,0:T(8,128)(2,1)S(1)} %get-tuple-element.11.l1_ref, bf16[152,144]{1,0:T(8,128)(2,1)S(1)} %get-tuple-element.12.l2_ref, bf16[16,16,128]{2,1,0:T(8,128)(2,1)S(1)} %get-tuple-element.13.unit_ref, f32[32,128]{1,0:T(8,128)S(1)} %get-tuple-element.14.front_ref, f32[512,128]{1,0:T(8,128)S(1)} %bitcast.7), custom_call_target="tpu_custom_call" | custom-call | tf_op jit(solution)/shard_map/speciate/pallas_call | solution.py:367
Async XLA Ops:
  0.0 12.6 %copy-start.2 = (f32[32,512]{1,0:T(8,128)S(1)}, f32[32,512]{1,0:T(8,128)}, u32[]{:S(2)}) copy-start(f32[32,512]{1,0:T(8,128)} %diff_ref.3) | copy-start | bytes 196612
  0.0 12.6 %copy-start.1 = (f32[32,512]{1,0:T(8,128)S(1)}, f32[32,512]{1,0:T(8,128)}, u32[]{:S(2)}) copy-start(f32[32,512]{1,0:T(8,128)} %cour_ref.3) | copy-start | bytes 196612
  0.0 12.6 %copy-start = (f32[4,32,512]{2,1,0:T(8,128)S(1)}, f32[4,32,512]{2,1,0:T(8,128)}, u32[]{:S(2)}) copy-start(f32[4,32,512]{2,1,0:T(8,128)} %tot_ref.3) | copy-start | bytes 786436
  1.1 9.8 %collective-permute-start = (f32[6,4,512]{2,1,0:T(4,128)S(1)}, f32[6,4,512]{2,1,0:T(4,128)S(1)}, u32[]{:S(2)}, u32[]{:S(2)}) collective-permute-start(f32[6,4,512]{2,1,0:T(4,128)S(1)} %get-tuple-element.15), channel_id=1, source_target_pairs={{0,4},{4,0},{8,12},{12,8},{16,20},{20,16},{24,28},{28,24},{32,36},... | collective-permute-start | bytes 147464 | tf_op jit(solution)/shard_map/ppermute | solution.py:390
  3.0 9.7 %collective-permute-start.1 = (f32[6,4,512]{2,1,0:T(4,128)S(1)}, f32[6,4,512]{2,1,0:T(4,128)S(1)}, u32[]{:S(2)}, u32[]{:S(2)}) collective-permute-start(f32[6,4,512]{2,1,0:T(4,128)S(1)} %get-tuple-element.16), channel_id=1, source_target_pairs={{4,8},{8,4},{12,16},{16,12},{20,24},{24,20},{28,32},{32,28},{36,40... | collective-permute-start | bytes 147464 | tf_op jit(solution)/shard_map/ppermute | solution.py:389
  14.1 10.1 %all-to-all-start = ((f32[4,128,128]{2,1,0:T(8,128)}), f32[4,128,128]{2,1,0:T(8,128)S(1)}, u32[]{:S(2)}, u32[]{:S(2)}) async-start(f32[4,128,128]{2,1,0:T(8,128)} %transport.1), calls=%async_computation | async-start | bytes 524288 | tf_op jit(solution)/shard_map/all_to_all | solution.py:392
